TPU v7x, 256 devices: a whole 4x4x8 slice. The times are simulated.
256 devices in a mesh: dp: 2 (over core), graph: 128 (over x, z, y).
Axes of the slice: x: 4, y: 4, z: 8, core: 2. Of those that a mesh axis runs over, the one named last changes fastest.
Arguments:
- features: bfloat16 [4096, 49, 128], P(('dp', 'graph')), may hold values from -6 to 6
- cotangent: bfloat16 [4096, 49, 128], P(('dp', 'graph')), may hold values from -0.029907227 to 0.029907227
- wigner: bfloat16 [256, 29, 49], replicated, may hold values from -2 to 2
- src_atom: int32 [32768], P(('dp', 'graph')), may hold values from 0 to 15
- dst_part: int32 [32768, 1], P(('dp', 'graph')), may hold values from 0 to 127; in each aligned block of 128 rows (0 to 127, 128 to 255, ...) at most 2 rows name the same one
- dst_atom: int32 [32768], P(('dp', 'graph')), may hold values from 0 to 15
- angle: int32 [32768], P(('dp', 'graph')), may hold values from 0 to 255
- w_zero: bfloat16 [896, 896], replicated, may hold values from -0.1875 to 0.1875
- w_one: bfloat16 [2, 768, 768], replicated, may hold values from -0.15625 to 0.15625
- w_two: bfloat16 [2, 640, 640], replicated, may hold values from -0.15625 to 0.15625
Outputs:
- aggregated: bfloat16 [4096, 49, 128], P(('dp', 'graph'))
- weight_grad: float32 [2801664], P('graph')
Inputs may be any that keep to these rules, and one draw needn't show every extreme that they name: `dst_part`: the edges of one device go to at most 2 per partition; in every draw some device sends exactly 2 edges to some partition.
All inputs are finite; a program needn't handle non-finite values.
Results may differ from a plain program's by a relative error of at most 0.0057.
Values may be sent and summed in bfloat16 or wider, within the bound.
A program may use at most 128 MiB of HBM per device.

v0:
```python
import jax
import jax.numpy as jnp
import numpy as np
from jax import lax
from jax.sharding import PartitionSpec as P

LMAX = 6
MMAX = 2


def kept_pairs():
    listing = []
    for azimuth in range(MMAX + 1):
        sign_list = [1] if azimuth == 0 else [1, -1]
        for sign_of in sign_list:
            for degree in range(azimuth, LMAX + 1):
                listing.append((degree, sign_of * azimuth))
    return listing


def degree_mask():
    full_degrees = np.repeat(np.arange(LMAX + 1), 2 * np.arange(LMAX + 1) + 1)
    kept_degrees = np.array([degree_pair[0] for degree_pair in kept_pairs()])
    return (kept_degrees[:, None] == full_degrees[None, :]).astype(np.float32)


def group_bounds():
    bounds = [(0, LMAX + 1)]
    offset = LMAX + 1
    for azimuth in range(1, MMAX + 1):
        length = LMAX + 1 - azimuth
        bounds.append((offset, length))
        bounds.append((offset + length, length))
        offset = offset + 2 * length
    return bounds


def flat_group(tile_rows, first_row, length):
    return tile_rows[:, first_row : first_row + length].reshape(
        tile_rows.shape[0], length * tile_rows.shape[2]
    )


def so2_mix(tile_rows, weights):
    bounds = group_bounds()
    count_rows = tile_rows.shape[0]
    channel_count = tile_rows.shape[2]
    zero_out = jnp.dot(
        flat_group(tile_rows, 0, LMAX + 1), weights[0], preferred_element_type=jnp.float32
    )
    pieces = [zero_out.reshape(count_rows, LMAX + 1, channel_count)]
    for azimuth in range(1, MMAX + 1):
        plus_start, length = bounds[2 * azimuth - 1]
        minus_start = bounds[2 * azimuth][0]
        plus_part = flat_group(tile_rows, plus_start, length)
        minus_part = flat_group(tile_rows, minus_start, length)
        real_w = weights[azimuth][0]
        imag_w = weights[azimuth][1]
        out_plus = jnp.dot(plus_part, real_w, preferred_element_type=jnp.float32) - jnp.dot(
            minus_part, imag_w, preferred_element_type=jnp.float32
        )
        out_minus = jnp.dot(plus_part, imag_w, preferred_element_type=jnp.float32) + jnp.dot(
            minus_part, real_w, preferred_element_type=jnp.float32
        )
        pieces.append(out_plus.reshape(count_rows, length, channel_count))
        pieces.append(out_minus.reshape(count_rows, length, channel_count))
    return jnp.concatenate(pieces, axis=1).astype(jnp.bfloat16)


def gram_matrix(left_rows, right_rows):
    return lax.dot_general(
        left_rows, right_rows, (((0,), (0,)), ((), ())), preferred_element_type=jnp.float32
    )


def so2_grads(tile_rows, grad_rows):
    bounds = group_bounds()
    flat_parts = [
        gram_matrix(flat_group(tile_rows, 0, LMAX + 1), flat_group(grad_rows, 0, LMAX + 1)).reshape(
            -1
        )
    ]
    for azimuth in range(1, MMAX + 1):
        plus_start, length = bounds[2 * azimuth - 1]
        minus_start = bounds[2 * azimuth][0]
        tile_plus = flat_group(tile_rows, plus_start, length)
        tile_minus = flat_group(tile_rows, minus_start, length)
        grad_plus = flat_group(grad_rows, plus_start, length)
        grad_minus = flat_group(grad_rows, minus_start, length)
        real_g = gram_matrix(tile_plus, grad_plus) + gram_matrix(tile_minus, grad_minus)
        imag_g = gram_matrix(tile_plus, grad_minus) - gram_matrix(tile_minus, grad_plus)
        flat_parts.append(jnp.stack([real_g, imag_g]).reshape(-1))
    return jnp.concatenate(flat_parts)


def shards(features, cotangent, wigner, src_atom, dst_part, dst_atom, angle, w_zero, w_one, w_two):
    weights = [w_zero, w_one, w_two]
    group_count = lax.axis_size("graph")
    atom_count = features.shape[0]
    coeff_count = features.shape[1]
    channel_count = features.shape[2]
    edge_count = src_atom.shape[0]
    kept_count = wigner.shape[1]
    capacity = 2 * edge_count // group_count
    slot_total = group_count * capacity
    wigner_table = wigner * jnp.asarray(degree_mask(), dtype=jnp.bfloat16)
    target = dst_part[:, 0]
    target_hot = (target[:, None] == jnp.arange(group_count, dtype=jnp.int32)[None, :]).astype(
        jnp.bfloat16
    )
    position = jnp.arange(edge_count, dtype=jnp.int32)
    before = (position[:, None] > position[None, :]).astype(jnp.bfloat16)
    earlier_count = jnp.dot(before, target_hot, preferred_element_type=jnp.float32)
    rank_value = jnp.sum(earlier_count * target_hot.astype(jnp.float32), axis=1)
    slot_index = target * capacity + rank_value.astype(jnp.int32)
    edge_code = angle * atom_count + dst_atom
    key_buffer = (
        jnp.full((slot_total,), -1, jnp.int32)
        .at[slot_index]
        .set(edge_code)
        .reshape(group_count, capacity)
    )
    arrived_keys = lax.all_to_all(
        key_buffer, "graph", split_axis=0, concat_axis=0, tiled=True
    ).reshape(slot_total)
    is_live = arrived_keys >= 0
    safe_code = jnp.where(is_live, arrived_keys, 0)
    slot_angle = safe_code // atom_count
    slot_atom = safe_code % atom_count
    slot_rotation = wigner_table[slot_angle]
    live_factor = is_live.astype(jnp.bfloat16)
    slot_upstream = cotangent[slot_atom] * live_factor[:, None, None]
    slot_pulled = jnp.einsum(
        "skj,sjc->skc", slot_rotation, slot_upstream, preferred_element_type=jnp.float32
    ).astype(jnp.bfloat16)
    edge_rotation = wigner_table[angle]
    source_x = features[src_atom]
    rotated = jnp.einsum(
        "ekj,ejc->ekc", edge_rotation, source_x, preferred_element_type=jnp.float32
    ).astype(jnp.bfloat16)
    message = so2_mix(rotated, weights)
    flat_rows = message.reshape(edge_count, kept_count * channel_count)
    buffer_rows = (
        jnp.zeros((slot_total, kept_count * channel_count), jnp.bfloat16)
        .at[slot_index]
        .set(flat_rows)
    )
    arrived = lax.all_to_all(
        buffer_rows.reshape(group_count, capacity, kept_count * channel_count),
        "graph",
        split_axis=0,
        concat_axis=0,
        tiled=True,
    )
    slot_message = arrived.reshape(slot_total, kept_count, channel_count)
    returned = lax.all_to_all(
        slot_pulled.reshape(group_count, capacity, kept_count * channel_count),
        "graph",
        split_axis=0,
        concat_axis=0,
        tiled=True,
    )
    edge_pulled = returned.reshape(slot_total, kept_count, channel_count)[slot_index]
    grad_terms = so2_grads(rotated, edge_pulled)
    returned_rows = jnp.einsum(
        "skj,skc->sjc", slot_rotation, slot_message, preferred_element_type=jnp.float32
    )
    atom_hot = (
        (slot_atom[None, :] == jnp.arange(atom_count, dtype=jnp.int32)[:, None]) & is_live[None, :]
    ).astype(jnp.float32)
    summed = jnp.dot(
        atom_hot,
        returned_rows.reshape(slot_total, coeff_count * channel_count),
        precision=lax.Precision.HIGHEST,
        preferred_element_type=jnp.float32,
    )
    aggregated = summed.reshape(atom_count, coeff_count, channel_count).astype(jnp.bfloat16)
    grad_share = lax.psum_scatter(grad_terms, "graph", scatter_dimension=0, tiled=True)
    weight_grad = lax.psum(grad_share, "dp")
    return (aggregated, weight_grad)


def solution(mesh):
    placed = (
        P(("dp", "graph"), None, None),
        P(("dp", "graph"), None, None),
        P(),
        P(("dp", "graph")),
        P(("dp", "graph"), None),
        P(("dp", "graph")),
        P(("dp", "graph")),
        P(),
        P(),
        P(),
    )
    return jax.shard_map(
        shards,
        mesh=mesh,
        in_specs=placed,
        out_specs=(P(("dp", "graph"), None, None), P("graph")),
        check_vma=False,
    )
```

profile of v0, /device:TPU:1, one launch (start us, length us, event | category | flops | bytes accessed | tf_op | source)
XLA Modules:
  0.0 554.8 jit_solution(11604445393256452863)
XLA Ops:
  11.2 16.3 %all-to-all-start = ((s32[128,1,2]{2,1,0:T(1,128)}), s32[128,1,2]{2,1,0:T(1,128)S(1)}, u32[]{:S(2)}, u32[]{:S(2)}) async-start(s32[128,1,2]{2,1,0:T(1,128)} %bitcast.3), calls=%async_computation | async-start | bytes 131072 | tf_op jit(solution)/shard_map/all_to_all | solution.py:123
  27.5 4.5 copy.46
  33.6 4.5 all-to-all-done
  39.7 2.6 gather_fusion
  42.3 14.8 %gather_fusion.3 = bf16[256,49,128]{2,0,1:T(8,128)(2,1)} fusion(bf16[16,49,128]{2,0,1:T(8,128)(2,1)S(1)} %copy-done, s32[1024]{0:T(1024)S(1)} %get-tuple-element.16), kind=kCustom, calls=%fused_computation.3 | custom fusion | bytes 6423552 | tf_op jit(solution)/shard_map/gather | solution.py:132
  59.4 4.3 fusion.4
  63.7 4.9 reshape.260
  68.6 9.4 %all-to-all-start.2 = ((bf16[128,2,3712]{2,1,0:T(2,128)(2,1)}), bf16[128,2,3712]{2,1,0:T(2,128)(2,1)}, u32[]{:S(2)}, u32[]{:S(2)}) async-start(bf16[128,2,3712]{2,1,0:T(2,128)(2,1)} %reshape.260), calls=%async_computation.2 | async-start | bytes 3801088 | tf_op jit(solution)/shard_map/all_to_all | solution.py:156
  78.1 3.3 gather_fusion.1
  81.3 8.0 %gather_fusion.2 = bf16[128,49,128]{2,0,1:T(8,128)(2,1)} fusion(bf16[16,49,128]{2,0,1:T(8,128)(2,1)S(1)} %copy-done.2, s32[1024]{0:T(1024)S(1)} %get-tuple-element.17), kind=kCustom, calls=%fused_computation.2 | custom fusion | bytes 3211776 | tf_op jit(solution)/shard_map/gather | solution.py:137
  89.4 3.1 fusion.9
  102.7 20.1 %all-to-all-done.2 = bf16[128,2,3712]{2,1,0:T(2,128)(2,1)} async-done(((bf16[128,2,3712]{2,1,0:T(2,128)(2,1)}), bf16[128,2,3712]{2,1,0:T(2,128)(2,1)}, u32[]{:S(2)}, u32[]{:S(2)}) %all-to-all-start.2) | async-done | bytes 1900576 | tf_op jit(solution)/shard_map/all_to_all | solution.py:156
  122.8 5.9 %reshape.261 = bf16[256,29,128]{2,1,0:T(8,128)(2,1)} reshape(bf16[128,2,3712]{2,1,0:T(2,128)(2,1)} %all-to-all-done.2) | data formatting | bytes 3801088 | tf_op jit(solution)/shard_map/reshape | solution.py:163
  128.7 2.4 gather_fusion.4
  142.6 4.5 reshape.269
  149.4 2.4 pad_maximum_fusion.1
  151.9 5.8 %reshape.266 = f32[1179648]{0:T(1024)} reshape(f32[2,768,768]{2,1,0:T(8,128)} %pad_maximum_fusion.1) | data formatting | bytes 9437184 | tf_op jit(solution)/shard_map/reshape | solution.py:92
  157.9 2.2 fusion.64
  160.1 4.5 reshape.263
  164.6 11.6 %pad_maximum_fusion = f32[2801664]{0:T(1024)} fusion(f32[819200]{0:T(1024)} %reshape.269, f32[1179648]{0:T(1024)} %reshape.266, f32[802816]{0:T(1024)} %reshape.263), kind=kLoop, calls=%fused_computation.7 | loop fusion | flops 5603328 | bytes 22413312 | tf_op jit(solution)/shard_map/concatenate | solution.py:93
  176.2 3.6 copy.49
  193.9 2.7 fusion.12
  201.2 3.5 scatter_custom_fusion.1
  204.8 4.9 reshape.257
  209.7 9.9 %all-to-all-start.1 = ((bf16[128,2,3712]{2,1,0:T(2,128)(2,1)}), bf16[128,2,3712]{2,1,0:T(2,128)(2,1)}, u32[]{:S(2)}, u32[]{:S(2)}) async-start(bf16[128,2,3712]{2,1,0:T(2,128)(2,1)} %reshape.257), calls=%async_computation.1 | async-start | bytes 3801088 | tf_op jit(solution)/shard_map/all_to_all | solution.py:148
  220.9 61.7 %all-to-all-done.1 = bf16[128,2,3712]{2,1,0:T(2,128)(2,1)} async-done(((bf16[128,2,3712]{2,1,0:T(2,128)(2,1)}), bf16[128,2,3712]{2,1,0:T(2,128)(2,1)}, u32[]{:S(2)}, u32[]{:S(2)}) %all-to-all-start.1) | async-done | bytes 1900576 | tf_op jit(solution)/shard_map/all_to_all | solution.py:148
  282.6 5.7 %reshape.258 = bf16[256,29,128]{2,1,0:T(8,128)(2,1)} reshape(bf16[128,2,3712]{2,1,0:T(2,128)(2,1)} %all-to-all-done.1) | data formatting | bytes 3801088 | tf_op jit(solution)/shard_map/reshape | solution.py:155
  288.3 6.9 %fusion.63 = f32[256,49,128]{2,1,0:T(8,128)} fusion(bf16[256,29,49]{2,1,0:T(8,128)(2,1)S(1)} %gather_fusion, bf16[256,29,128]{2,1,0:T(8,128)(2,1)} %reshape.258), kind=kOutput, calls=%fused_computation.103 | convolution fusion | flops 93126656 | bytes 9050624 | tf_op jit(solution)/shard_map/skj,skc->sjc/dot_general | solution.py:165
  295.3 8.4 %copy.60 = f32[256,49,128]{0,2,1:T(8,128)} copy(f32[256,49,128]{2,1,0:T(8,128)} %fusion.63) | data formatting | bytes 12845056 | tf_op jit(solution)/shard_map/skj,skc->sjc/dot_general | solution.py:165
  303.7 207.0 %all-reduce.6.cloned.1.call-done = f32[2801664]{0:T(1024)} async-done(((f32[2801664]{0:T(1024)}), f32[2801664]{0:T(1024)}) %all-reduce.6.cloned.1.call-update) | async-done | bytes 11206672
  512.3 6.6 %fusion.13 = bf16[16,49,128]{2,0,1:T(8,128)(2,1)} fusion(f32[256,49,128]{0,2,1:T(8,128)} %copy.60, s32[256]{0:T(256)S(1)} %and_select_fusion.2, pred[256]{0:T(512)(128)(4,1)S(1)} %get-tuple-element.13), kind=kOutput, calls=%fused_computation.29 | convolution fusion | flops 308389888 | bytes 6624512 | tf_op jit(solution)/shard_map/dot_general | solution.py:171
  518.9 27.3 %all-reduce.4.cloned.1.call-done = f32[21888]{0:T(1024)} async-done(((f32[21888]{0:T(1024)}), f32[21888]{0:T(1024)}) %all-reduce.4.cloned.1.call-update) | async-done | bytes 87568 | tf_op jit(solution)/shard_map/psum | solution.py:179
  (104 shorter events, 56.1 us)
Async XLA Ops:
  7.2 35.2 %copy-start = (bf16[16,49,128]{2,0,1:T(8,128)(2,1)S(1)}, bf16[16,49,128]{2,0,1:T(8,128)(2,1)}, u32[]{:S(2)}) copy-start(bf16[16,49,128]{2,0,1:T(8,128)(2,1)} %param.12) | copy-start | bytes 602116
  7.2 24.9 %copy-start.13 = (bf16[29,49]{1,0:T(8,128)(2,1)S(1)}, bf16[29,49]{1,0:T(8,128)(2,1)}, u32[]{:S(2)}) copy-start(bf16[29,49]{1,0:T(8,128)(2,1)} %constant.47.clone) | copy-start | bytes 8530
  8.8 72.6 %copy-start.14 = (s32[128]{0:T(128)}, s32[128]{0:T(128)S(1)}, u32[]{:S(2)}) copy-start(s32[128]{0:T(128)S(1)} %fusion.55) | copy-start | bytes 1540
  11.2 26.9 %all-to-all-start = ((s32[128,1,2]{2,1,0:T(1,128)}), s32[128,1,2]{2,1,0:T(1,128)S(1)}, u32[]{:S(2)}, u32[]{:S(2)}) async-start(s32[128,1,2]{2,1,0:T(1,128)} %bitcast.3), calls=%async_computation | async-start | bytes 131072 | tf_op jit(solution)/shard_map/all_to_all | solution.py:123
  32.1 1.5 copy-start.15
  68.6 12.7 %copy-start.2 = (bf16[16,49,128]{2,0,1:T(8,128)(2,1)S(1)}, bf16[16,49,128]{2,0,1:T(8,128)(2,1)}, u32[]{:S(2)}) copy-start(bf16[16,49,128]{2,0,1:T(8,128)(2,1)} %param.11) | copy-start | bytes 602116
  68.6 54.2 %all-to-all-start.2 = ((bf16[128,2,3712]{2,1,0:T(2,128)(2,1)}), bf16[128,2,3712]{2,1,0:T(2,128)(2,1)}, u32[]{:S(2)}, u32[]{:S(2)}) async-start(bf16[128,2,3712]{2,1,0:T(2,128)(2,1)} %reshape.260), calls=%async_computation.2 | async-start | bytes 3801088 | tf_op jit(solution)/shard_map/all_to_all | solution.py:156
  78.0 432.7 %all-reduce.6.cloned.1.call-start = ((), (), s32[]{:S(2)}) async-start(), calls=%async_computation.4 | async-start | bytes 22413312
  131.1 6.9 %copy-start.3 = (bf16[128,29,128]{2,1,0:T(8,128)(2,1)}, bf16[128,29,128]{2,1,0:T(8,128)(2,1)S(1)}, u32[]{:S(2)}) copy-start(bf16[128,29,128]{2,1,0:T(8,128)(2,1)S(1)} %gather_fusion.4) | copy-start | bytes 2850820
  136.6 2.8 copy-start.4
  136.6 2.8 copy-start.9
  139.4 0.9 copy-start.8
  142.6 4.5 copy-start.11
  142.6 4.7 copy-start.10
  151.9 5.8 %slice-start = ((bf16[128,29,128]{2,1,0:T(8,128)(2,1)}), bf16[128,7,128]{2,1,0:T(8,128)(2,1)S(1)}, s32[]{:S(2)}) async-start(bf16[128,29,128]{2,1,0:T(8,128)(2,1)} %copy-done.3), calls=%async_computation.5 | async-start | bytes 524288 | tf_op jit(solution)/shard_map/slice | solution.py:39
  151.9 6.0 %copy-start.7 = (bf16[128,7,128]{0,2,1:T(8,128)(2,1)S(1)}, bf16[128,7,128]{0,2,1:T(8,128)(2,1)}, u32[]{:S(2)}) copy-start(bf16[128,7,128]{0,2,1:T(8,128)(2,1)} %copy.48) | copy-start | bytes 688132
  183.8 3.7 copy-start.6
  185.7 3.4 copy-start.5
  192.2 4.4 copy-start.12
  209.7 10.0 %copy-start.16 = (u32[256]{0:T(256)S(1)}, u32[256]{0:T(256)}, u32[]{:S(2)}) copy-start(u32[256]{0:T(256)} %constant.56) | copy-start | bytes 3076
  209.7 73.0 %all-to-all-start.1 = ((bf16[128,2,3712]{2,1,0:T(2,128)(2,1)}), bf16[128,2,3712]{2,1,0:T(2,128)(2,1)}, u32[]{:S(2)}, u32[]{:S(2)}) async-start(bf16[128,2,3712]{2,1,0:T(2,128)(2,1)} %reshape.257), calls=%async_computation.1 | async-start | bytes 3801088 | tf_op jit(solution)/shard_map/all_to_all | solution.py:148
  219.6 326.6 %all-reduce.4.cloned.1.call-start = ((), (), s32[]{:S(2)}) async-start(), calls=%async_computation.3 | async-start | bytes 180224 | tf_op jit(solution)/shard_map/psum | solution.py:179
  512.3 35.4 %copy-start.1 = (bf16[16,49,128]{2,0,1:T(8,128)(2,1)S(1)}, bf16[16,49,128]{2,0,1:T(8,128)(2,1)}, u32[]{:S(2)}) copy-start(bf16[16,49,128]{2,0,1:T(8,128)(2,1)} %param.12) | copy-start | bytes 602116
Sparse Core Ops, SparseCore 0:
  176.3 334.3 all-reduce.5
  513.8 32.3 all-reduce.3
where the time goes:
time: 560 us; the launch traced here: 555 us
  waiting for transfers between devices  321 us (57%)
  local copies, waits for them, and re-layouts  116 us (21%)
  matrix products  44.9 us (8%)
  starting transfers between devices  35.7 us (6%)
  other arithmetic  21.8 us (4%)
  between operations  15.4 us (3%)
    unnamed x3, waiting for transfers between devices  207 us
    all_to_all x1, waiting for transfers between devices, shards(): lax.all_to_all(buffer_rows.reshape(group_count, capacity, kept_count * ch...  61.7 us
    psum x1, waiting for transfers between devices, shards(): weight_grad = lax.psum(grad_share, 'dp')  27.3 us
    all_to_all x1, waiting for transfers between devices, shards(): lax.all_to_all(slot_pulled.reshape(group_count, capacity, kept_count * ch...  20.1 us
    slice x17, local copies, waits for them, and re-layouts, flat_group(): tile_rows[:, first_row:first_row + length]  16.4 us
    all_to_all x1, starting transfers between devices, shards(): lax.all_to_all(key_buffer, 'graph', split_axis=0, concat_axis=0, tiled=True)  16.3 us
    gather x1, local copies, waits for them, and re-layouts, shards(): slot_upstream = cotangent[slot_atom] * live_factor[:, None, None]  14.8 us
    unnamed x42, local copies, waits for them, and re-layouts  14.5 us
  transfers between devices with their start and end apart: 5, of which 5 were waited for; matrix products, arithmetic and copies ran while one was open for 17% of the time, Pallas kernels for 0%

commit v1 on v0

v1 whole, which is shorter than its diff:
```python
import functools

import jax
import jax.numpy as jnp
from jax import lax
from jax.experimental import pallas as pl
from jax.experimental.pallas import tpu as pltpu
from jax.sharding import PartitionSpec as P

LMAX = 6
MMAX = 2
NX, NZ, NY = 4, 8, 4
NXY = NX * NY
EDGES = 128
ATOMS = 16
SLOTS = 256
ROWS = 21888
SHARD = 171
QUART = 48
MESH = pl.DeviceIdType.MESH
BF = jnp.bfloat16
F32 = jnp.float32


def kept_degrees():
    out = list(range(LMAX + 1))
    for m in range(1, MMAX + 1):
        for _ in range(2):
            out.extend(range(m, LMAX + 1))
    return out


DEGREE = kept_degrees()
KEPT = len(DEGREE)
WIRE = KEPT + 2
GROUPS = [(0, 7), (7, 6), (13, 6), (19, 5), (24, 5)]


def width(degree):
    return 128 if degree <= 3 else 256


def dot(a, b):
    return jnp.dot(a, b, preferred_element_type=F32)


def iota(shape, dim):
    return lax.broadcasted_iota(jnp.int32, shape, dim)


def remote(src, dst, send, recv, device):
    return pltpu.make_async_remote_copy(
        src_ref=src, dst_ref=dst, send_sem=send, recv_sem=recv, device_id=device, device_id_type=MESH
    )


def build_table(wig, table):
    for degree in range(LMAX + 1):
        w = width(degree)
        j = iota((128, w), 0)
        n = iota((128, w), 1)
        spread = ((j == degree * degree + n // ATOMS) & (n < ATOMS * (2 * degree + 1))).astype(BF)
        for k in [k for k in range(KEPT) if DEGREE[k] == degree]:
            table[k, :, 0:w] = dot(wig[k], spread).astype(BF)


def build_rotation(angle, atom, table, left):
    lane = iota((SLOTS, 128), 1)
    near = (angle == lane.astype(F32)).astype(BF)
    far = (angle == (lane + 128).astype(F32)).astype(BF)
    pick = jnp.concatenate([near, far], axis=1)
    mask = (atom == (lane % ATOMS + 1).astype(F32)).astype(F32)
    wide = jnp.concatenate([mask, mask], axis=1)
    for k in range(KEPT):
        w = width(DEGREE[k])
        gate = mask if w == 128 else wide
        left[k, :, 0:w] = (dot(pick, table[k, :, 0:w]) * gate).astype(BF)


def kernel(
    tgt, src, dat, ang, wig, feat, cot, w0, w1, w2,
    agg, wgrad,
    table, left, mycode, codes, fall, cpad, sendb, recvb, pull, xt, flat,
    pk, r0, sa, sb, ra, ta, rb, rc, sa1, sb1, ra1, ta1, rb1, rc1, sa2, sb2, r3, fin,
    code_s, code_r, ring_s, ring_r, ex_s, ex_r, loc_s, dp_s, dp_r, st_s, st_r, z_s, z_r, f_s, f_r,
):
    dp = lax.axis_index("dp")
    g = lax.axis_index("graph")
    x = g // 32
    z = (g // 4) % 8
    y = g % 4
    xy = x * 4 + y

    def at(px, pz, py):
        return (dp, px * 32 + pz * 4 + py)

    partner = (1 - dp, g)

    def zpeer(i):
        return lax.rem(z + i, NZ)

    def xypeer(i):
        return lax.rem(xy + i, NXY)

    barrier = pltpu.get_barrier_semaphore()

    def greet_z(i, c):
        pl.semaphore_signal(barrier, inc=1, device_id=at(x, zpeer(i), y), device_id_type=MESH)
        return c

    def greet_xy(i, c):
        q = xypeer(i)
        pl.semaphore_signal(barrier, inc=1, device_id=at(q // 4, z, q % 4), device_id_type=MESH)
        return c

    lax.fori_loop(1, NZ, greet_z, 0)
    lax.fori_loop(1, NXY, greet_xy, 0)
    pl.semaphore_signal(barrier, inc=1, device_id=partner, device_id_type=MESH)

    trow = jnp.broadcast_to(tgt[...], (EDGES, EDGES)).astype(F32)
    tcol = jnp.transpose(trow)
    earlier = (tcol == trow) & (iota((EDGES, EDGES), 0) < iota((EDGES, EDGES), 1))
    rank = jnp.sum(earlier.astype(F32), axis=0, keepdims=True).astype(jnp.int32)
    t = tgt[...]
    pos = ((t >> 2) & 7) * 32 + ((t >> 5) * 4 + (t & 3)) * 2 + rank
    hot = (iota((SLOTS, EDGES), 0) == jnp.broadcast_to(pos, (SLOTS, EDGES))).astype(BF)
    for i, row in enumerate([ang[...], src[...] + 1, dat[...] + 1]):
        wide = jnp.broadcast_to(row, (EDGES, EDGES)).astype(F32).astype(BF)
        got = lax.dot_general(hot, wide, (((1,), (1,)), ((), ())), preferred_element_type=F32)
        mycode[:, i] = got.astype(BF).reshape(NZ, 32, 128)

    fall[z, 0:784] = feat[...]
    for q in range(NZ):
        fall[q, 784:832] = jnp.zeros((48, 128), BF)
    pl.semaphore_wait(barrier, 23)

    sign = 1 - 2 * dp

    def ring(step_sem, block, direction):
        dev = at(x, lax.rem(z + direction + NZ, NZ), y)
        part = fall.at[block, pl.ds(0, 784)]
        return remote(part, part, ring_s.at[step_sem], ring_r.at[step_sem], dev)

    def behind(n):
        return lax.rem(z - sign * n + 2 * NZ, NZ)

    def ahead(n):
        return lax.rem(z + sign * n + 2 * NZ, NZ)

    ring(0, z, sign).start()
    ring(4, z, -sign).start()

    def code_copy(i):
        q = zpeer(i)
        return remote(mycode.at[q], codes.at[z], code_s.at[i], code_r.at[i], at(x, q, y))

    def send_code(i, c):
        code_copy(i).start()
        return c

    def wait_code(i, c):
        code_copy(i).wait()
        return c

    lax.fori_loop(1, NZ, send_code, 0)
    codes[z] = mycode[z]
    build_table(wig, table)
    lax.fori_loop(1, NZ, wait_code, 0)
    build_rotation(
        codes[:, 0].reshape(SLOTS, 128).astype(F32), codes[:, 1].reshape(SLOTS, 128).astype(F32), table, left
    )

    def exchange(step, zz, i):
        q = xypeer(i)
        return remote(
            sendb.at[step, :, q], recvb.at[:, zz, xy], ex_s.at[step, i], ex_r.at[step, i], at(q // 4, z, q % 4)
        )

    def own_copy(step, zz):
        return pltpu.make_async_copy(sendb.at[step, :, xy], recvb.at[:, zz, xy], loc_s.at[step])

    def rotate(step, zz):
        rows = pl.ds(pl.multiple_of(zz * 32, 32), 32)
        for degree in range(LMAX + 1):
            w = width(degree)
            ks = [k for k in range(KEPT) if DEGREE[k] == degree]
            lhs = jnp.concatenate([left[k, rows, 0:w] for k in ks], axis=0)
            lo = ATOMS * degree * degree
            got = dot(lhs, fall[zz, lo : lo + w]).astype(BF)
            for i, k in enumerate(ks):
                sendb[step, k] = got[32 * i : 32 * i + 32].reshape(NXY, 2, 128)
        sendb[step, KEPT] = codes[zz, 0].reshape(NXY, 2, 128)
        sendb[step, KEPT + 1] = codes[zz, 2].reshape(NXY, 2, 128)

        def go(i, c):
            exchange(step, zz, i).start()
            return c

        lax.fori_loop(1, NXY, go, 0)
        own_copy(step, zz).start()

    order = [z]
    for n in range(1, 5):
        order.append(behind(n))
        if n < 4:
            order.append(ahead(n))
    for step in range(NZ):
        n = (step + 1) // 2
        if step % 2 == 1:
            ring(n - 1, behind(n), sign).wait_recv()
            if n < 4:
                ring(n, behind(n), sign).start()
        elif step:
            ring(3 + n, ahead(n), -sign).wait_recv()
            if n < 3:
                ring(4 + n, ahead(n), -sign).start()
        rotate(step, order[step])
    for n in range(4):
        ring(n, z, sign).wait_send()
    for n in range(3):
        ring(4 + n, z, -sign).wait_send()

    for step in range(NZ):

        def done(i, c):
            exchange(step, order[step], i).wait()
            return c

        lax.fori_loop(1, NXY, done, 0)
        own_copy(step, order[step]).wait()

    def rot(k):
        return recvb[k].reshape(SLOTS, 128)

    build_rotation(rot(KEPT).astype(F32), rot(KEPT + 1).astype(F32), table, left)
    cpad[0:784] = cot[...]
    cpad[784:832] = jnp.zeros((48, 128), BF)
    for k in range(KEPT):
        w = width(DEGREE[k])
        lo = ATOMS * DEGREE[k] * DEGREE[k]
        pull[k] = dot(left[k, :, 0:w], cpad[lo : lo + w]).astype(BF)
        xt[k] = jnp.transpose(rot(k).astype(F32)).astype(BF)

    def cat(ks):
        return jnp.concatenate([rot(k) for k in ks], axis=1)

    message = {}
    zero = dot(cat(range(7)), w0[...]).astype(BF)
    for i in range(7):
        message[i] = zero[:, 128 * i : 128 * i + 128]
    for m, w in ((1, w1), (2, w2)):
        plus, length = GROUPS[2 * m - 1]
        minus = GROUPS[2 * m][0]
        p, q = cat(range(plus, plus + length)), cat(range(minus, minus + length))
        up = (dot(p, w[0]) - dot(q, w[1])).astype(BF)
        um = (dot(p, w[1]) + dot(q, w[0])).astype(BF)
        for i in range(length):
            message[plus + i] = up[:, 128 * i : 128 * i + 128]
            message[minus + i] = um[:, 128 * i : 128 * i + 128]
    for degree in range(LMAX + 1):
        w = width(degree)
        ks = [k for k in range(KEPT) if DEGREE[k] == degree]
        lhs = jnp.concatenate([left[k, :, 0:w] for k in ks], axis=0)
        rhs = jnp.concatenate([message[k] for k in ks], axis=0)
        got = lax.dot_general(lhs, rhs, (((0,), (0,)), ((), ())), preferred_element_type=F32)
        size = 2 * degree + 1
        agg[degree * degree : (degree + 1) * (degree + 1)] = (
            got[0 : ATOMS * size].astype(BF).reshape(size, ATOMS, 128)
        )

    def spread(res, base, length, lo, width_):
        for jb in range(lo, lo + width_):
            flat[pl.ds(base + jb, 128 * length, stride=length), :] = res[:, 128 * (jb - lo) : 128 * (jb - lo) + 128]

    zt = jnp.concatenate([xt[k] for k in range(7)], axis=0)
    for lo in range(0, 7, 2):
        n = min(2, 7 - lo)
        rhs = jnp.concatenate([pull[lo + i] for i in range(n)], axis=1)
        spread(dot(zt, rhs), 0, 7, lo, n)
    base = 896 * 7
    for m in (1, 2):
        plus, length = GROUPS[2 * m - 1]
        minus = GROUPS[2 * m][0]
        pqt = jnp.concatenate(
            [jnp.concatenate([xt[plus + i], xt[minus + i]], axis=1) for i in range(length)], axis=0
        )
        for lo in range(0, length, 2):
            n = min(2, length - lo)
            gg = jnp.concatenate([pull[plus + lo + i] for i in range(n)], axis=1)
            hh = jnp.concatenate([pull[minus + lo + i] for i in range(n)], axis=1)
            spread(dot(pqt, jnp.concatenate([gg, hh], axis=0)), base, length, lo, n)
            spread(dot(pqt, jnp.concatenate([hh, -gg], axis=0)), base + 128 * length * length, length, lo, n)
        base += 2 * 128 * length * length
    flat[ROWS : ROWS + 24] = jnp.zeros((24, 128), F32)

    def pack(s, c):
        for a in range(2):
            pk[a, s] = flat[pl.ds(SHARD * s + QUART * (2 * (1 - dp) + a), QUART), :].astype(BF)
        return c

    lax.fori_loop(0, 128, pack, 0)
    swap = remote(pk, r0, dp_s, dp_r, partner)
    swap.start()
    swap.wait()

    def merge(s, c):
        sx = s // 32
        sz = (s // 4) % 8
        sy = s % 4
        sa[sx, sy, sz] = (flat[pl.ds(SHARD * s + QUART * 2 * dp, QUART), :] + r0[0, s].astype(F32)).astype(BF)
        sb[sy, sx, sz] = (flat[pl.ds(SHARD * s + QUART * (2 * dp + 1), QUART), :] + r0[1, s].astype(F32)).astype(BF)
        return c

    lax.fori_loop(0, 128, merge, 0)

    def along_x(d):
        return at(lax.rem(x + d + NX, NX), z, y)

    def along_y(d):
        return at(x, z, lax.rem(y + d + NY, NY))

    def stage(number, parts):
        chains = []
        for i, (p, move, s, r_a, t_a, r_b, r_c, out) in enumerate(parts):

            def chunk(d, s=s, p=p):
                return s.at[lax.rem(p + d + 4, 4)]

            first = remote(chunk(2 * sign), r_a, st_s.at[number, i, 0], st_r.at[number, i, 0], move(sign))
            second = remote(chunk(-sign), r_b, st_s.at[number, i, 1], st_r.at[number, i, 1], move(-sign))
            third = remote(t_a, r_c, st_s.at[number, i, 2], st_r.at[number, i, 2], move(sign))
            first.start()
            second.start()
            chains.append((first, second, third, chunk))
        for (p, move, s, r_a, t_a, r_b, r_c, out), (first, second, third, chunk) in zip(parts, chains):
            first.wait_recv()
            t_a[...] = (r_a[...].astype(F32) + chunk(sign)[...].astype(F32)).astype(BF)
            third.start()
        for (p, move, s, r_a, t_a, r_b, r_c, out), (first, second, third, chunk) in zip(parts, chains):
            second.wait_recv()
            third.wait_recv()
            out[...] = (chunk(0)[...].astype(F32) + r_b[...].astype(F32) + r_c[...].astype(F32)).astype(BF)
            first.wait_send()
            second.wait_send()
            third.wait_send()

    stage(
        0,
        [
            (x, along_x, sa, ra.at[0], ta.at[0], rb.at[0], rc.at[0], sa1),
            (y, along_y, sb, ra.at[1], ta.at[1], rb.at[1], rc.at[1], sb1),
        ],
    )
    stage(
        1,
        [
            (y, along_y, sa1, ra1.at[0], ta1.at[0], rb1.at[0], rc1.at[0], sa2),
            (x, along_x, sb1, ra1.at[1], ta1.at[1], rb1.at[1], rc1.at[1], sb2),
        ],
    )

    for a, s2 in ((0, sa2), (1, sb2)):

        def zcopy(i, s2=s2, a=a):
            q = zpeer(i)
            return remote(s2.at[q], r3.at[a, i], z_s.at[a, i], z_r.at[a, i], at(x, q, y))

        def zgo(i, c):
            zcopy(i).start()
            return c

        lax.fori_loop(1, NZ, zgo, 0)
    for a, s2 in ((0, sa2), (1, sb2)):
        total = s2[z].astype(F32)
        for i in range(1, NZ):
            remote(s2.at[zpeer(i)], r3.at[a, i], z_s.at[a, i], z_r.at[a, i], at(x, zpeer(i), y)).wait()
            total = total + r3[a, i].astype(F32)
        fin[2 * dp + a] = total
    last = remote(fin.at[pl.ds(2 * dp, 2)], fin.at[pl.ds(2 * dp, 2)], f_s, f_r, partner)
    last.start()
    last.wait()
    for q in range(4):
        n = min(QUART, SHARD - QUART * q)
        wgrad[QUART * q : QUART * q + n] = fin[q, 0:n]


def shards(features, cotangent, wigner, src_atom, dst_part, dst_atom, angle, w_zero, w_one, w_two):
    feat = jnp.transpose(features, (1, 0, 2)).reshape(784, 128)
    cot = jnp.transpose(cotangent, (1, 0, 2)).reshape(784, 128)
    wig = jnp.pad(jnp.transpose(wigner, (1, 0, 2)), ((0, 0), (0, 0), (0, 128 - 49)))
    dma = pltpu.SemaphoreType.DMA
    chunk = (32, QUART, 128)
    scratch = [
        pltpu.VMEM((KEPT, SLOTS, 256), BF),
        pltpu.VMEM((KEPT, SLOTS, 256), BF),
        pltpu.VMEM((NZ, 3, 32, 128), BF),
        pltpu.VMEM((NZ, 3, 32, 128), BF),
        pltpu.VMEM((NZ, 832, 128), BF),
        pltpu.VMEM((832, 128), BF),
        pltpu.VMEM((NZ, WIRE, NXY, 2, 128), BF),
        pltpu.VMEM((WIRE, NZ, NXY, 2, 128), BF),
        pltpu.VMEM((KEPT, SLOTS, 128), BF),
        pltpu.VMEM((KEPT, 128, SLOTS), BF),
        pltpu.VMEM((ROWS + 24, 128), F32),
        pltpu.VMEM((2, 128, QUART, 128), BF),
        pltpu.VMEM((2, 128, QUART, 128), BF),
        pltpu.VMEM((NX, NY, NZ, QUART, 128), BF),
        pltpu.VMEM((NY, NX, NZ, QUART, 128), BF),
    ]
    for lead in ((4, NZ), (NZ,)):
        scratch += [pltpu.VMEM((2,) + lead + (QUART, 128), BF) for _ in range(4)]
        scratch += [pltpu.VMEM(lead + (QUART, 128), BF) for _ in range(2)]
    scratch += [
        pltpu.VMEM((2, NZ, QUART, 128), BF),
        pltpu.VMEM((4, QUART, 128), F32),
        dma((NZ,)), dma((NZ,)),
        dma((7,)), dma((7,)),
        dma((NZ, NXY)), dma((NZ, NXY)), dma((NZ,)),
        dma, dma,
        dma((2, 2, 3)), dma((2, 2, 3)),
        dma((2, NZ)), dma((2, NZ)),
        dma, dma,
    ]
    vmem = pl.BlockSpec(memory_space=pltpu.VMEM)
    agg, wgrad = pl.pallas_call(
        kernel,
        out_shape=(
            jax.ShapeDtypeStruct((49, ATOMS, 128), BF),
            jax.ShapeDtypeStruct((SHARD, 128), F32),
        ),
        in_specs=[vmem] * 10,
        out_specs=(vmem, vmem),
        scratch_shapes=scratch,
        compiler_params=pltpu.CompilerParams(
            collective_id=0, has_side_effects=True, vmem_limit_bytes=67000000
        ),
    )(
        dst_part.reshape(1, EDGES),
        src_atom.reshape(1, EDGES),
        dst_atom.reshape(1, EDGES),
        angle.reshape(1, EDGES),
        wig, feat, cot, w_zero, w_one, w_two,
    )
    return jnp.transpose(agg, (1, 0, 2)), wgrad.reshape(SHARD * 128)


def solution(mesh):
    both = ("dp", "graph")
    placed = (
        P(both, None, None), P(both, None, None), P(), P(both), P(both, None), P(both), P(both), P(), P(), P(),
    )
    return jax.shard_map(
        shards,
        mesh=mesh,
        in_specs=placed,
        out_specs=(P(both, None, None), P("graph")),
        check_vma=False,
    )
```

time: 560 us -> 114 us (0.20)
  waiting for transfers between devices: 321 us -> 0 us
  local copies, waits for them, and re-layouts: 116 us -> 7.1 us
  Pallas kernels: 0 us -> 106 us
  matrix products: 44.9 us -> 0 us
  starting transfers between devices: 35.7 us -> 0 us
  other arithmetic: 21.8 us -> 0 us
  between operations: 15.4 us -> 0.65 us
    unnamed x3 -> x0, waiting for transfers between devices: 207 us -> none
    pallas_call x0 -> x1, Pallas kernels: none -> 106 us  [shards(): pl.pallas_call(kernel, out_shape=(jax.ShapeDtypeStruct((49, ATOMS, 128),...]
    all_to_all x3 -> x0, waiting for transfers between devices: 86.3 us -> none  [the longest x1 61.7 us: shards(): lax.all_to_all(buffer_rows.reshape(group_count, capacity, kept_count * ch...]
    dot_general x23 -> x0, matrix products: 44.9 us -> none  [the longest x9 7.64 us: gram_matrix(): lax.dot_general(left_rows, right_rows, (((0,), (0,)), ((), ())), preferre...]
    reshape x9 -> x0, local copies, waits for them, and re-layouts: 36.4 us -> none  [the longest x2 10.3 us: so2_grads(): flat_parts.append(jnp.stack([real_g, imag_g]).reshape(-1))]
    all_to_all x3 -> x0, starting transfers between devices: 35.6 us -> none  [the longest x1 16.3 us: shards(): lax.all_to_all(key_buffer, 'graph', split_axis=0, concat_axis=0, tiled=True)]
    gather x5 -> x0, local copies, waits for them, and re-layouts: 31.1 us -> none  [the longest x1 14.8 us: shards(): slot_upstream = cotangent[slot_atom] * live_factor[:, None, None]]
    psum x1 -> x0, waiting for transfers between devices: 27.3 us -> none  [shards(): weight_grad = lax.psum(grad_share, 'dp')]
  transfers between devices with their start and end apart: 5 -> 0, of which waited for: 5 -> 0; matrix products, arithmetic and copies ran while one was open for 17% -> 0% of each run, Pallas kernels for 0% -> 0%
where the time goes in v1:
time: 114 us; the launch traced here: 113 us
  Pallas kernels  106 us (93%)
  local copies, waits for them, and re-layouts  7.1 us (6%)
    pallas_call x1, Pallas kernels, shards(): pl.pallas_call(kernel, out_shape=(jax.ShapeDtypeStruct((49, ATOMS, 128),...  106 us
    unnamed x3, local copies, waits for them, and re-layouts  5.36 us

profile of v1, /device:TPU:1, one launch (start us, length us, event | category | flops | bytes accessed | tf_op | source)
XLA Modules:
  0.0 113.5 jit_solution(8725072156872676008)
XLA Ops:
  0.6 2.2 %copy.12 = bf16[256,29,49]{2,0,1:T(8,128)(2,1)S(1)} copy(bf16[256,29,49]{0,1,2:T(8,128)(2,1)} %param.12) | data formatting | bytes 1455104 | tf_op args[2]
  2.8 1.7 %pad.4.wig = bf16[29,256,128]{2,1,0:T(8,128)(2,1)} pad(bf16[29,256,49]{2,1,0:T(8,128)(2,1)S(1)} %bitcast.13, bf16[]{:T(256)} %constant.2.clone.1), padding=0_0x0_0x0_79 | pad | bytes 2628098 | tf_op jit(solution)/shard_map/jit(_pad)/pad | solution.py:390
  4.6 105.7 %shard_map.113 = (bf16[49,16,128]{2,1,0:T(8,128)(2,1)}, f32[171,128]{1,0:T(8,128)}) custom-call(s32[1,128]{1,0:T(1,128)} %bitcast.18, s32[1,128]{1,0:T(1,128)} %bitcast.19, s32[1,128]{1,0:T(1,128)} %bitcast.20, s32[1,128]{1,0:T(1,128)} %bitcast.21, bf16[29,256,128]{2,1,0:T(8,128)(2,1)} %pad.4.wig, bf16[784,128]{1,0:T(8,128)(2,1)} %bitcast.14, ...), custom_call_target="tpu_custom_call" | custom-call | tf_op jit(solution)/shard_map/pallas_call | solution.py:425
  110.3 1.6 %copy.15 = bf16[16,49,128]{2,0,1:T(8,128)(2,1)} copy(bf16[16,49,128]{2,0,1:T(8,128)(2,1)} %bitcast.16) | data formatting | bytes 401408
  111.9 1.5 %copy.16 = f32[21888]{0:T(1024)} copy(f32[21888]{0:T(1024)} %bitcast.17) | data formatting | bytes 175104

commit v2 on v1

v2 whole, which is shorter than its diff:
```python
import functools

import jax
import jax.numpy as jnp
from jax import lax
from jax.experimental import pallas as pl
from jax.experimental.pallas import tpu as pltpu
from jax.sharding import PartitionSpec as P

LMAX = 6
MMAX = 2
NX, NZ, NY = 4, 8, 4
NXY = NX * NY
EDGES = 128
ATOMS = 16
SLOTS = 256
ROWS = 21888
SHARD = 171
HALF = 88
RING = 32
REST = 24
MESH = pl.DeviceIdType.MESH
BF = jnp.bfloat16
F32 = jnp.float32


def kept_degrees():
    out = list(range(LMAX + 1))
    for m in range(1, MMAX + 1):
        for _ in range(2):
            out.extend(range(m, LMAX + 1))
    return out


DEGREE = kept_degrees()
KEPT = len(DEGREE)
WIRE = KEPT + 2
SPLIT = 21
CODE = SPLIT - 2
BY_DEGREE = sorted(range(KEPT), key=lambda k: (DEGREE[k], k))
PLACE = {k: i if i < CODE else i + 2 for i, k in enumerate(BY_DEGREE)}
GROUPS = [(0, 7), (7, 6), (13, 6), (19, 5), (24, 5)]


def width(degree):
    return 128 if degree <= 3 else 256


def dot(a, b):
    return jnp.dot(a, b, preferred_element_type=F32)


def iota(shape, dim):
    return lax.broadcasted_iota(jnp.int32, shape, dim)


def remote(src, dst, send, recv, device):
    return pltpu.make_async_remote_copy(
        src_ref=src, dst_ref=dst, send_sem=send, recv_sem=recv, device_id=device, device_id_type=MESH
    )


def build_table(wig, wk, table):
    wk[...] = jnp.zeros_like(wk)
    wk[:, 0:49, :] = jnp.swapaxes(wig[...].astype(F32), 0, 1).astype(BF)
    for degree in range(LMAX + 1):
        w = width(degree)
        j = iota((w, 64), 1)
        n = iota((w, 64), 0)
        spread = ((j == degree * degree + n // ATOMS) & (n < ATOMS * (2 * degree + 1))).astype(BF)
        for k in [k for k in range(KEPT) if DEGREE[k] == degree]:
            table[k, 0:w] = dot(spread, wk[k]).astype(BF)


def build_rotation(angle, atom, table, left, rows):
    size = angle.shape[0]
    lane = iota((size, 128), 1)
    near = (angle == lane.astype(F32)).astype(BF)
    far = (angle == (lane + 128).astype(F32)).astype(BF)
    pick = jnp.concatenate([near, far], axis=1)
    mask = (atom == (lane % ATOMS + 1).astype(F32)).astype(F32)
    wide = jnp.concatenate([mask, mask], axis=1)
    for k in range(KEPT):
        w = width(DEGREE[k])
        gate = mask if w == 128 else wide
        got = lax.dot_general(pick, table[k, 0:w], (((1,), (1,)), ((), ())), preferred_element_type=F32)
        got = (got * gate).astype(BF)
        step = size // len(rows)
        for i, part in enumerate(rows):
            left[k, part, 0:w] = got[step * i : step * i + step]


def kernel(
    tgt, src, dat, ang, wig_in, feat, cot, w0_in, w1_in, w2_in,
    agg, wgrad,
    wig, w0, w1, w2, table, wk, left, leftd, crow, codes, fall, cpad, sendb, recvb, pull, xt, flat,
    pk, r0, s0, ra, ta, rb, rc, s1, ra1, ta1, rb1, rc1, s2, r3, fin,
    sz, ua, va, ub, vb, sz1, r4,
    code_s, code_r, ring_s, ring_r, ex_s, ex_r, loc_s, dp_s, dp_r, st_s, st_r, su_s, su_r, z_s, z_r, f_s, f_r, in_s,
    ua_s, ua_r, ub_s, ub_r, w_s, w_r,
):
    dp = lax.axis_index("dp")
    g = lax.axis_index("graph")
    x = g // 32
    z = (g // 4) % 8
    y = g % 4
    xy = x * 4 + y
    sign = 1 - 2 * dp

    def at(px, pz, py):
        return (dp, px * 32 + pz * 4 + py)

    partner = (1 - dp, g)

    def zpeer(i):
        return lax.rem(z + i, NZ)

    def xypeer(i):
        return lax.rem(xy + i, NXY)

    barrier = pltpu.get_barrier_semaphore()

    def greet_z(i, c):
        pl.semaphore_signal(barrier, inc=1, device_id=at(x, zpeer(i), y), device_id_type=MESH)
        return c

    def greet_xy(i, c):
        q = xypeer(i)
        pl.semaphore_signal(barrier, inc=1, device_id=at(q // 4, z, q % 4), device_id_type=MESH)
        return c

    lax.fori_loop(1, NZ, greet_z, 0)
    lax.fori_loop(1, NXY, greet_xy, 0)
    pl.semaphore_signal(barrier, inc=1, device_id=partner, device_id_type=MESH)

    loads = [
        pltpu.make_async_copy(a, b, in_s.at[i])
        for i, (a, b) in enumerate(
            [
                (wig_in, wig), (feat, fall.at[z, pl.ds(0, 784)]), (cot, cpad.at[pl.ds(0, 784)]),
                (w0_in, w0), (w1_in, w1), (w2_in, w2),
            ]
        )
    ]
    for load in loads:
        load.start()

    trow = jnp.broadcast_to(tgt[...], (EDGES, EDGES)).astype(F32)
    tcol = jnp.transpose(trow)
    earlier = (tcol == trow) & (iota((EDGES, EDGES), 0) < iota((EDGES, EDGES), 1))
    rank = jnp.sum(earlier.astype(F32), axis=0, keepdims=True).astype(jnp.int32)
    t = tgt[...]
    pos = ((t >> 2) & 7) * 32 + ((t >> 5) * 4 + (t & 3)) * 2 + rank
    line = iota((16, EDGES), 0)
    code = jnp.zeros((16, EDGES), jnp.int32)
    for i, row in enumerate([pos, ang[...], src[...] + 1, dat[...] + 1]):
        code = jnp.where(line == i, jnp.broadcast_to(row, (16, EDGES)), code)
    crow[z] = code.astype(F32).astype(BF)

    def expand(q):
        c = crow[q].astype(F32)
        hot = (iota((32, EDGES), 0) + 32 * z).astype(F32) == jnp.broadcast_to(c[0:1], (32, EDGES))
        wide = jnp.concatenate([jnp.broadcast_to(c[i : i + 1], (EDGES, EDGES)) for i in (1, 2, 3)], axis=0)
        got = lax.dot_general(
            hot.astype(BF), wide.astype(BF), (((1,), (1,)), ((), ())), preferred_element_type=F32
        )
        for i in range(3):
            codes[q, i] = got[:, 128 * i : 128 * i + 128].astype(BF)

    for q in range(NZ):
        fall[q, 784:832] = jnp.zeros((48, 128), BF)
    loads[0].wait()
    build_table(wig, wk, table)
    expand(z)
    mine = pl.ds(pl.multiple_of(z * 32, 32), 32)
    build_rotation(codes[z, 0].astype(F32), codes[z, 1].astype(F32), table, left, [mine])

    def exchange(step, piece, i):
        q = xypeer(i)
        part = pl.ds(0, SPLIT) if piece == 0 else pl.ds(SPLIT, WIRE - SPLIT)
        return remote(
            sendb.at[step, part, q], recvb.at[part, step, xy], ex_s.at[step], ex_r.at[step], at(q // 4, z, q % 4)
        )

    def own_copy(step):
        return pltpu.make_async_copy(sendb.at[step, :, xy], recvb.at[:, step, xy], loc_s.at[step])

    def rotate(step, piece, zz):
        rows = pl.ds(pl.multiple_of(zz * 32, 32), 32)
        for degree in range(5) if piece == 0 else range(5, LMAX + 1):
            w = width(degree)
            ks = [k for k in range(KEPT) if DEGREE[k] == degree]
            lhs = jnp.concatenate([left[k, rows, 0:w] for k in ks], axis=0)
            lo = ATOMS * degree * degree
            if piece == 0:
                w = min(w, 400 - lo)
                lhs = lhs[:, 0:w]
            got = dot(lhs, fall[zz, lo : lo + w]).astype(BF)
            for i, k in enumerate(ks):
                sendb[step, PLACE[k]] = got[32 * i : 32 * i + 32].reshape(NXY, 2, 128)
        if piece == 0:
            sendb[step, CODE] = codes[zz, 0].reshape(NXY, 2, 128)
            sendb[step, CODE + 1] = codes[zz, 2].reshape(NXY, 2, 128)

    def send_block(step, piece):
        def go(i, c):
            exchange(step, piece, i).start()
            return c

        lax.fori_loop(1, NXY, go, 0)
        if piece:
            own_copy(step).start()

    def whole(step):
        part = recvb.at[:, step, pl.ds(0, NXY - 1)]
        return remote(part, part, ex_s.at[step], ex_r.at[step], at(x, z, y))

    def receive_block(step):
        whole(step).wait_recv()
        own_copy(step).wait()

    loads[1].wait()
    rotate(0, 0, z)
    rotate(0, 1, z)
    pl.semaphore_wait(barrier, 23)

    def code_copy(i):
        return remote(crow.at[z], crow.at[z], code_s.at[i], code_r.at[i], at(x, zpeer(i), y))

    def code_in(i):
        q = lax.rem(z - i + NZ, NZ)
        return remote(crow.at[q], crow.at[q], code_s.at[i], code_r.at[i], at(x, zpeer(i), y))

    def send_code(i, c):
        code_copy(i).start()
        return c

    def wait_code(i, c):
        code_in(i).wait_recv()
        return c

    def sent_code(i, c):
        code_copy(i).wait_send()
        return c

    lax.fori_loop(1, NZ, send_code, 0)

    def ring(hop, piece, block, direction):
        dev = at(x, lax.rem(z + direction + NZ, NZ), y)
        part = fall.at[block, pl.ds(400 * piece, 400 - 16 * piece)]
        return remote(part, part, ring_s.at[hop, piece], ring_r.at[hop, piece], dev)

    def behind(n):
        return lax.rem(z - sign * n + 2 * NZ, NZ)

    def ahead(n):
        return lax.rem(z + sign * n + 2 * NZ, NZ)

    for piece in range(2):
        ring(0, piece, z, sign).start()
    send_block(0, 0)
    send_block(0, 1)
    cpad[784:832] = jnp.zeros((48, 128), BF)

    def prepare(blocks):
        for q in blocks:
            expand(q)
        rows = [pl.ds(pl.multiple_of(q * 32, 32), 32) for q in blocks]
        build_rotation(
            jnp.concatenate([codes[q, 0] for q in blocks], axis=0).astype(F32),
            jnp.concatenate([codes[q, 1] for q in blocks], axis=0).astype(F32),
            table, left, rows,
        )

    def half(h):
        rows = pl.ds(128 * h, 128)

        def rot(k):
            return recvb[k, 4 * h : 4 * h + 4].reshape(128, 128)

        build_rotation(rot(CODE).astype(F32), rot(CODE + 1).astype(F32), table, leftd, [rows])
        for k in range(KEPT):
            w = width(DEGREE[k])
            lo = ATOMS * DEGREE[k] * DEGREE[k]
            pull[k, rows] = dot(leftd[k, rows, 0:w], cpad[lo : lo + w]).astype(BF)
            xt[k, :, rows] = jnp.transpose(rot(PLACE[k]).astype(F32)).astype(BF)

    def pass_on(n, piece, back):
        if back:
            ring(n - 1, piece, behind(n), sign).wait_recv()
            if n < 4:
                ring(n, piece, behind(n), sign).start()
        elif n < 4:
            ring(3 + n, piece, ahead(n), -sign).wait_recv()
            if n < 3:
                ring(4 + n, piece, ahead(n), -sign).start()

    code_in(1).wait_recv()
    code_in(NZ - 1).wait_recv()
    prepare([behind(1), ahead(1)])
    for piece in range(2):
        ring(4, piece, z, -sign).start()
    for n in range(1, 5):
        for back in (True, False):
            if n == 4 and not back:
                break
            step = 2 * n - 1 if back else 2 * n
            for piece in range(2):
                pass_on(n, piece, back)
                if n == 2 and back and piece == 0:
                    lax.fori_loop(2, NZ - 1, wait_code, 0)
                    prepare([behind(2), ahead(2), behind(3), ahead(3), behind(4)])
                rotate(step, piece, behind(n) if back else ahead(n))
                send_block(step, piece)
    loads[2].wait()
    for early in range(4):
        receive_block(early)
    half(0)
    for late in range(4, NZ):
        receive_block(late)
    half(1)

    def spread(res, base, length, lo, width_):
        for jb in range(lo, lo + width_):
            flat[pl.ds(base + jb, 128 * length, stride=length), :] = res[:, 128 * (jb - lo) : 128 * (jb - lo) + 128]

    def grads(m):
        if m == 0:
            zt = jnp.concatenate([xt[k] for k in range(7)], axis=0)
            for lo in range(0, 7, 2):
                n = min(2, 7 - lo)
                rhs = jnp.concatenate([pull[lo + i] for i in range(n)], axis=1)
                spread(dot(zt, rhs), 0, 7, lo, n)
            return
        base = 128 * (49 if m == 1 else 49 + 72)
        plus, length = GROUPS[2 * m - 1]
        minus = GROUPS[2 * m][0]
        pqt = jnp.concatenate(
            [jnp.concatenate([xt[plus + i], xt[minus + i]], axis=1) for i in range(length)], axis=0
        )
        for lo in range(0, length, 2):
            n = min(2, length - lo)
            gg = jnp.concatenate([pull[plus + lo + i] for i in range(n)], axis=1)
            hh = jnp.concatenate([pull[minus + lo + i] for i in range(n)], axis=1)
            spread(dot(pqt, jnp.concatenate([gg, hh], axis=0)), base, length, lo, n)
            spread(dot(pqt, jnp.concatenate([hh, -gg], axis=0)), base + 128 * length * length, length, lo, n)

    def pack(s, c):
        pk[s] = flat[pl.ds(SHARD * s + HALF * (1 - dp), HALF), :].astype(BF)
        return c

    def merge(s, c):
        sx = s // 32
        cz = (s // 4) % 8
        sy = s % 4
        both = (flat[pl.ds(SHARD * s + HALF * dp, HALF), :] + r0[s].astype(F32)).astype(BF)
        s0[0, sx, sy, cz] = both[0:RING]
        s0[1, sy, sx, cz] = both[RING : 2 * RING]
        sz[cz, sx * 4 + sy] = both[2 * RING : HALF]
        return c

    flat[ROWS : ROWS + 24] = jnp.zeros((24, 128), F32)
    runs = [(0, 36), (36, 90), (90, 128)]
    swaps = []
    for m, (lo, hi) in enumerate(runs):
        grads(m)
        lax.fori_loop(lo, hi, pack, 0)
        part = pl.ds(lo, hi - lo)
        swaps.append(remote(pk.at[part], r0.at[part], dp_s.at[m], dp_r.at[m], partner))
        swaps[m].start()
    for m, (lo, hi) in enumerate(runs):
        swaps[m].wait()
        lax.fori_loop(lo, hi, merge, 0)

    def mixed(k):
        return recvb[k].reshape(SLOTS, 128)

    def cat(ks):
        return jnp.concatenate([mixed(PLACE[k]) for k in ks], axis=1)

    message = {}

    def mix(m):
        if m == 0:
            zero = dot(cat(range(7)), w0[...]).astype(BF)
            for i in range(7):
                message[i] = zero[:, 128 * i : 128 * i + 128]
            return
        w = w1 if m == 1 else w2
        plus, length = GROUPS[2 * m - 1]
        minus = GROUPS[2 * m][0]
        p, q = cat(range(plus, plus + length)), cat(range(minus, minus + length))
        up = (dot(p, w[0]) - dot(q, w[1])).astype(BF)
        um = (dot(p, w[1]) + dot(q, w[0])).astype(BF)
        for i in range(length):
            message[plus + i] = up[:, 128 * i : 128 * i + 128]
            message[minus + i] = um[:, 128 * i : 128 * i + 128]

    def gather_atoms():
        for degree in range(LMAX + 1):
            w = width(degree)
            ks = [k for k in range(KEPT) if DEGREE[k] == degree]
            lhs = jnp.concatenate([leftd[k, :, 0:w] for k in ks], axis=0)
            rhs = jnp.concatenate([message[k] for k in ks], axis=0)
            got = lax.dot_general(lhs, rhs, (((0,), (0,)), ((), ())), preferred_element_type=F32)
            size = 2 * degree + 1
            agg[degree * degree : (degree + 1) * (degree + 1)] = (
                got[0 : ATOMS * size].astype(BF).reshape(size, ATOMS, 128)
            )

    def along_x(d):
        return at(lax.rem(x + d + NX, NX), z, y)

    def along_y(d):
        return at(x, z, lax.rem(y + d + NY, NY))

    def mod4(v):
        return lax.rem(v + 4, 4)

    parts = [(0, x, along_x, y, along_y), (1, y, along_y, x, along_x)]
    one, two, three, subs = [], [], [], []
    for i, p, move, q, _ in parts:
        order = [mod4(q + 2 * sign), mod4(q - sign), mod4(q + sign), q]
        subs.append(order)
        one.append(
            [remote(s0.at[i, mod4(p + 2 * sign), j], ra.at[i, j], st_s.at[i, 0, n], st_r.at[i, 0, n], move(sign))
             for n, j in enumerate(order)]
        )
        two.append(
            [remote(s0.at[i, mod4(p - sign), j], rb.at[i, j], st_s.at[i, 1, n], st_r.at[i, 1, n], move(-sign))
             for n, j in enumerate(order)]
        )
        three.append(
            [remote(ta.at[i, j], rc.at[i, j], st_s.at[i, 2, n], st_r.at[i, 2, n], move(sign))
             for n, j in enumerate(order)]
        )
    def mod8(v):
        return lax.rem(v + 8, 8)

    def up(h, j):
        src = sz.at[mod8(z + 4 * sign), pl.ds(8 * j, 8)] if h == 0 else va.at[h - 1, j]
        return remote(src, ua.at[h, j], ua_s.at[h, j], ua_r.at[h, j], at(x, mod8(z + sign), y))

    def down(h, j):
        src = sz.at[mod8(z - 3 * sign), pl.ds(8 * j, 8)] if h == 0 else vb.at[h - 1, j]
        return remote(src, ub.at[h, j], ub_s.at[h, j], ub_r.at[h, j], at(x, mod8(z - sign), y))

    def pass_sum(h, j):
        part = pl.ds(8 * j, 8)
        up(h, j).wait_recv()
        va[h, j] = (ua[h, j].astype(F32) + sz[mod8(z + (3 - h) * sign), part].astype(F32)).astype(BF)
        up(h + 1, j).start()
        if h < 2:
            down(h, j).wait_recv()
            vb[h, j] = (ub[h, j].astype(F32) + sz[mod8(z - (2 - h) * sign), part].astype(F32)).astype(BF)
            down(h + 1, j).start()

    def end_sum(j):
        part = pl.ds(8 * j, 8)
        up(3, j).wait_recv()
        down(2, j).wait_recv()
        sz1[part] = (sz[z, part].astype(F32) + ua[3, j].astype(F32) + ub[2, j].astype(F32)).astype(BF)

    def relay(n):
        for i, p, *_ in parts:
            j = subs[i][n]
            one[i][n].wait_recv()
            ta[i, j] = (ra[i, j].astype(F32) + s0[i, mod4(p + sign), j].astype(F32)).astype(BF)
            three[i][n].start()

    four, five, six = [], [], []
    for i, p, _, q, move in parts:
        order = subs[i]
        four.append(remote(s1.at[i, order[0]], ra1.at[i], su_s.at[i, 0], su_r.at[i, 0], move(sign)))
        five.append(remote(s1.at[i, order[1]], rb1.at[i], su_s.at[i, 1], su_r.at[i, 1], move(-sign)))
        six.append(remote(ta1.at[i], rc1.at[i], su_s.at[i, 2], su_r.at[i, 2], move(sign)))

    def close(n):
        for i, p, *_ in parts:
            j = subs[i][n]
            two[i][n].wait_recv()
            three[i][n].wait_recv()
            s1[i, j] = (s0[i, p, j].astype(F32) + rb[i, j].astype(F32) + rc[i, j].astype(F32)).astype(BF)
            if n == 0:
                four[i].start()
            if n == 1:
                five[i].start()

    for j in range(2):
        up(0, j).start()
        down(0, j).start()
    for n in range(4):
        for i in range(2):
            one[i][n].start()
            two[i][n].start()
    for load in loads[3:]:
        load.wait()
    mix(1)
    pass_sum(0, 0)
    relay(0)
    pass_sum(0, 1)
    relay(1)
    mix(0)
    pass_sum(1, 0)
    relay(2)
    pass_sum(1, 1)
    relay(3)
    mix(2)
    pass_sum(2, 0)
    close(0)
    pass_sum(2, 1)
    for n in range(1, 4):
        close(n)
    for i in range(2):
        four[i].wait_recv()
        ta1[i] = (ra1[i].astype(F32) + s1[i, subs[i][2]].astype(F32)).astype(BF)
        six[i].start()
    for j in range(2):
        end_sum(j)

    def across(i):
        q = xypeer(i)
        return remote(sz1.at[q], r4.at[i], w_s.at[i], w_r.at[i], at(q // 4, z, q % 4))

    def across_go(i, c):
        across(i).start()
        return c

    lax.fori_loop(1, NXY, across_go, 0)
    gather_atoms()
    for i in range(2):
        five[i].wait_recv()
        six[i].wait_recv()
        s2[i] = (s1[i, subs[i][3]].astype(F32) + rb1[i].astype(F32) + rc1[i].astype(F32)).astype(BF)

    def zcopy(a, i):
        q = zpeer(i)
        return remote(s2.at[a, q], r3.at[a, i], z_s.at[a, i], z_r.at[a, i], at(x, q, y))

    for a in range(2):

        def zgo(i, c):
            zcopy(a, i).start()
            return c

        lax.fori_loop(1, NZ, zgo, 0)
    total = sz1[xy].astype(F32)
    for i in range(1, NXY):
        across(i).wait()
        total = total + r4[i].astype(F32)
    fin[dp, 2 * RING : HALF] = total
    for a in range(2):
        total = s2[a, z].astype(F32)
        for i in range(1, NZ):
            zcopy(a, i).wait()
            total = total + r3[a, i].astype(F32)
        fin[dp, RING * a : RING * a + RING] = total
    last = remote(fin.at[dp], fin.at[dp], f_s, f_r, partner)
    last.start()
    for j in range(2):
        for h in range(4):
            up(h, j).wait_send()
        for h in range(3):
            down(h, j).wait_send()
    for n in range(4):
        for i in range(2):
            one[i][n].wait_send()
            two[i][n].wait_send()
            three[i][n].wait_send()
    for i in range(2):
        four[i].wait_send()
        five[i].wait_send()
        six[i].wait_send()
    for piece in range(2):
        for n in range(4):
            ring(n, piece, z, sign).wait_send()
        for n in range(3):
            ring(4 + n, piece, z, -sign).wait_send()
    for step in range(NZ):
        whole(step).wait_send()
    lax.fori_loop(1, NZ, sent_code, 0)
    last.wait()
    wgrad[0:HALF] = fin[0]
    wgrad[HALF:SHARD] = fin[1, 0 : SHARD - HALF]


def shards(features, cotangent, wigner, src_atom, dst_part, dst_atom, angle, w_zero, w_one, w_two):
    dma = pltpu.SemaphoreType.DMA
    scratch = [
        pltpu.VMEM((49, KEPT, 256), BF),
        pltpu.VMEM(w_zero.shape, BF),
        pltpu.VMEM(w_one.shape, BF),
        pltpu.VMEM(w_two.shape, BF),
        pltpu.VMEM((KEPT, SLOTS, 256), BF),
        pltpu.VMEM((KEPT, 64, 256), BF),
        pltpu.VMEM((KEPT, SLOTS, 256), BF),
        pltpu.VMEM((KEPT, SLOTS, 256), BF),
        pltpu.VMEM((NZ, 16, 128), BF),
        pltpu.VMEM((NZ, 3, 32, 128), BF),
        pltpu.VMEM((NZ, 832, 128), BF),
        pltpu.VMEM((832, 128), BF),
        pltpu.VMEM((NZ, WIRE, NXY, 2, 128), BF),
        pltpu.VMEM((WIRE, NZ, NXY, 2, 128), BF),
        pltpu.VMEM((KEPT, SLOTS, 128), BF),
        pltpu.VMEM((KEPT, 128, SLOTS), BF),
        pltpu.VMEM((ROWS + 24, 128), F32),
        pltpu.VMEM((128, HALF, 128), BF),
        pltpu.VMEM((128, HALF, 128), BF),
        pltpu.VMEM((2, 4, 4, NZ, RING, 128), BF),
    ]
    scratch += [pltpu.VMEM((2, 4, NZ, RING, 128), BF) for _ in range(4)]
    scratch += [pltpu.VMEM((2, 4, NZ, RING, 128), BF)]
    scratch += [pltpu.VMEM((2, NZ, RING, 128), BF) for _ in range(4)]
    scratch += [pltpu.VMEM((2, NZ, RING, 128), BF)]
    scratch += [
        pltpu.VMEM((2, NZ, RING, 128), BF),
        pltpu.VMEM((2, HALF, 128), F32),
        pltpu.VMEM((NZ, NXY, REST, 128), BF),
        pltpu.VMEM((4, 2, 8, REST, 128), BF),
        pltpu.VMEM((3, 2, 8, REST, 128), BF),
        pltpu.VMEM((3, 2, 8, REST, 128), BF),
        pltpu.VMEM((2, 2, 8, REST, 128), BF),
        pltpu.VMEM((NXY, REST, 128), BF),
        pltpu.VMEM((NXY, REST, 128), BF),
        dma((NZ,)), dma((NZ,)),
        dma((7, 2)), dma((7, 2)),
        dma((NZ,)), dma((NZ,)), dma((NZ,)),
        dma((3,)), dma((3,)),
        dma((2, 3, 4)), dma((2, 3, 4)),
        dma((2, 3)), dma((2, 3)),
        dma((2, NZ)), dma((2, NZ)),
        dma, dma,
        dma((6,)),
        dma((4, 2)), dma((4, 2)), dma((3, 2)), dma((3, 2)), dma((NXY,)), dma((NXY,)),
    ]
    vmem = pl.BlockSpec(memory_space=pltpu.VMEM)
    agg, wgrad = pl.pallas_call(
        kernel,
        out_shape=(
            jax.ShapeDtypeStruct((49, ATOMS, 128), BF),
            jax.ShapeDtypeStruct((SHARD, 128), F32),
        ),
        in_specs=[vmem] * 4 + [pl.BlockSpec(memory_space=pl.ANY)] * 6,
        out_specs=(vmem, vmem),
        scratch_shapes=scratch,
        compiler_params=pltpu.CompilerParams(
            collective_id=0, has_side_effects=True, vmem_limit_bytes=67000000
        ),
    )(
        dst_part.reshape(1, EDGES),
        src_atom.reshape(1, EDGES),
        dst_atom.reshape(1, EDGES),
        angle.reshape(1, EDGES),
        jnp.transpose(wigner, (2, 1, 0)),
        jnp.transpose(features, (1, 0, 2)).reshape(784, 128),
        jnp.transpose(cotangent, (1, 0, 2)).reshape(784, 128),
        w_zero, w_one, w_two,
    )
    return jnp.transpose(agg, (1, 0, 2)), wgrad.reshape(SHARD * 128)


def solution(mesh):
    both = ("dp", "graph")
    placed = (
        P(both, None, None), P(both, None, None), P(), P(both), P(both, None), P(both), P(both), P(), P(), P(),
    )
    return jax.shard_map(
        shards,
        mesh=mesh,
        in_specs=placed,
        out_specs=(P(both, None, None), P("graph")),
        check_vma=False,
    )
```

time: 114 us -> 80.6 us (0.71)
  Pallas kernels: 106 us -> 76.6 us
  local copies, waits for them, and re-layouts: 7.1 us -> 3.15 us
    pallas_call x1, Pallas kernels: 106 us -> 76.6 us  [shards(): pl.pallas_call(kernel, out_shape=(jax.ShapeDtypeStruct((49, ATOMS, 128),...]
    unnamed x3 -> x2, local copies, waits for them, and re-layouts: 5.36 us -> 3.15 us
    pad x1 -> x0, local copies, waits for them, and re-layouts: 1.74 us -> none  [shards(): jnp.pad(jnp.transpose(wigner, (1, 0, 2)), ((0, 0), (0, 0), (0, 128 - 49)))]
where the time goes in v2:
time: 80.6 us; the launch traced here: 80.4 us
  Pallas kernels  76.6 us (95%)
  local copies, waits for them, and re-layouts  3.15 us (4%)
    pallas_call x1, Pallas kernels, shards(): pl.pallas_call(kernel, out_shape=(jax.ShapeDtypeStruct((49, ATOMS, 128),...  76.6 us
    unnamed x2, local copies, waits for them, and re-layouts  3.15 us

profile of v2, /device:TPU:1, one launch (start us, length us, event | category | flops | bytes accessed | tf_op | source)
XLA Modules:
  0.0 80.4 jit_solution(1731162384301458214)
XLA Ops:
  0.6 76.6 %shard_map.113 = (bf16[49,16,128]{2,1,0:T(8,128)(2,1)}, f32[171,128]{1,0:T(8,128)}) custom-call(s32[1,128]{1,0:T(1,128)} %bitcast.18, s32[1,128]{1,0:T(1,128)} %bitcast.19, s32[1,128]{1,0:T(1,128)} %bitcast.20, s32[1,128]{1,0:T(1,128)} %bitcast.21, bf16[49,29,256]{2,1,0:T(8,128)(2,1)} %bitcast.13, bf16[784,128]{1,0:T(8,128)(2,1)} %bitcast.14, ...), custom_call_target="tpu_custom_call" | custom-call | tf_op jit(solution)/shard_map/pallas_call | solution.py:637
  77.3 1.6 %copy.14 = bf16[16,49,128]{2,0,1:T(8,128)(2,1)} copy(bf16[16,49,128]{2,0,1:T(8,128)(2,1)} %bitcast.16) | data formatting | bytes 401408
  78.9 1.5 %copy.15 = f32[21888]{0:T(1024)} copy(f32[21888]{0:T(1024)} %bitcast.17) | data formatting | bytes 175104

commit v3 on v2

--- a/solution.py
+++ b/solution.py
@@ -92,11 +92,11 @@
 
 def kernel(
     tgt, src, dat, ang, wig_in, feat, cot, w0_in, w1_in, w2_in,
-    agg, wgrad,
-    wig, w0, w1, w2, table, wk, left, leftd, crow, codes, fall, cpad, sendb, recvb, pull, xt, flat,
+    agg_out, wgrad,
+    agg, wig, w0, w1, w2, table, wk, left, leftd, crow, codes, fall, cpad, sendb, recvb, pull, xt, flat,
     pk, r0, s0, ra, ta, rb, rc, s1, ra1, ta1, rb1, rc1, s2, r3, fin,
     sz, ua, va, ub, vb, sz1, r4,
-    code_s, code_r, ring_s, ring_r, ex_s, ex_r, loc_s, dp_s, dp_r, st_s, st_r, su_s, su_r, z_s, z_r, f_s, f_r, in_s,
+    code_s, code_r, ring_s, ring_r, ex_s, ex_r, loc_s, dp_s, dp_r, st_s, st_r, su_s, su_r, z_s, z_r, f_s, f_r, in_s, out_s,
     ua_s, ua_r, ub_s, ub_r, w_s, w_r,
 ):
     dp = lax.axis_index("dp")
@@ -169,11 +169,6 @@
 
     for q in range(NZ):
         fall[q, 784:832] = jnp.zeros((48, 128), BF)
-    loads[0].wait()
-    build_table(wig, wk, table)
-    expand(z)
-    mine = pl.ds(pl.multiple_of(z * 32, 32), 32)
-    build_rotation(codes[z, 0].astype(F32), codes[z, 1].astype(F32), table, left, [mine])
 
     def exchange(step, piece, i):
         q = xypeer(i)
@@ -220,8 +215,6 @@
         own_copy(step).wait()
 
     loads[1].wait()
-    rotate(0, 0, z)
-    rotate(0, 1, z)
     pl.semaphore_wait(barrier, 23)
 
     def code_copy(i):
@@ -258,8 +251,16 @@
 
     for piece in range(2):
         ring(0, piece, z, sign).start()
-    send_block(0, 0)
-    send_block(0, 1)
+    loads[0].wait()
+    build_table(wig, wk, table)
+    for piece in range(2):
+        ring(4, piece, z, -sign).start()
+    expand(z)
+    mine = pl.ds(pl.multiple_of(z * 32, 32), 32)
+    build_rotation(codes[z, 0].astype(F32), codes[z, 1].astype(F32), table, left, [mine])
+    for piece in range(2):
+        rotate(0, piece, z)
+        send_block(0, piece)
     cpad[784:832] = jnp.zeros((48, 128), BF)
 
     def prepare(blocks):
@@ -298,8 +299,6 @@
     code_in(1).wait_recv()
     code_in(NZ - 1).wait_recv()
     prepare([behind(1), ahead(1)])
-    for piece in range(2):
-        ring(4, piece, z, -sign).start()
     for n in range(1, 5):
         for back in (True, False):
             if n == 4 and not back:
@@ -496,6 +495,7 @@
     for load in loads[3:]:
         load.wait()
     mix(1)
+    mix(2)
     pass_sum(0, 0)
     relay(0)
     pass_sum(0, 1)
@@ -505,7 +505,6 @@
     relay(2)
     pass_sum(1, 1)
     relay(3)
-    mix(2)
     pass_sum(2, 0)
     close(0)
     pass_sum(2, 1)
@@ -528,6 +527,8 @@
 
     lax.fori_loop(1, NXY, across_go, 0)
     gather_atoms()
+    store_agg = pltpu.make_async_copy(agg, agg_out, out_s.at[0])
+    store_agg.start()
     for i in range(2):
         five[i].wait_recv()
         six[i].wait_recv()
@@ -548,15 +549,18 @@
     for i in range(1, NXY):
         across(i).wait()
         total = total + r4[i].astype(F32)
-    fin[dp, 2 * RING : HALF] = total
+    fin[2 * RING : HALF] = total
     for a in range(2):
         total = s2[a, z].astype(F32)
         for i in range(1, NZ):
             zcopy(a, i).wait()
             total = total + r3[a, i].astype(F32)
-        fin[dp, RING * a : RING * a + RING] = total
-    last = remote(fin.at[dp], fin.at[dp], f_s, f_r, partner)
+        fin[RING * a : RING * a + RING] = total
+    mine = wgrad.at[pl.ds(pl.multiple_of(HALF * dp, 8), HALF)]
+    last = remote(fin, mine, f_s, f_r, partner)
     last.start()
+    store = pltpu.make_async_copy(fin, mine, out_s.at[1])
+    store.start()
     for j in range(2):
         for h in range(4):
             up(h, j).wait_send()
@@ -579,14 +583,20 @@
     for step in range(NZ):
         whole(step).wait_send()
     lax.fori_loop(1, NZ, sent_code, 0)
+    store_agg.wait()
+    store.wait()
     last.wait()
-    wgrad[0:HALF] = fin[0]
-    wgrad[HALF:SHARD] = fin[1, 0 : SHARD - HALF]
+
+
+def finish(agg_in, wgrad_in, agg, wgrad):
+    agg[...] = agg_in[...]
+    wgrad[...] = wgrad_in[0:SHARD]
 
 
 def shards(features, cotangent, wigner, src_atom, dst_part, dst_atom, angle, w_zero, w_one, w_two):
     dma = pltpu.SemaphoreType.DMA
     scratch = [
+        pltpu.VMEM((49, ATOMS, 128), BF),
         pltpu.VMEM((49, KEPT, 256), BF),
         pltpu.VMEM(w_zero.shape, BF),
         pltpu.VMEM(w_one.shape, BF),
@@ -614,7 +624,7 @@
     scratch += [pltpu.VMEM((2, NZ, RING, 128), BF)]
     scratch += [
         pltpu.VMEM((2, NZ, RING, 128), BF),
-        pltpu.VMEM((2, HALF, 128), F32),
+        pltpu.VMEM((HALF, 128), F32),
         pltpu.VMEM((NZ, NXY, REST, 128), BF),
         pltpu.VMEM((4, 2, 8, REST, 128), BF),
         pltpu.VMEM((3, 2, 8, REST, 128), BF),
@@ -630,7 +640,7 @@
         dma((2, 3)), dma((2, 3)),
         dma((2, NZ)), dma((2, NZ)),
         dma, dma,
-        dma((6,)),
+        dma((6,)), dma((2,)),
         dma((4, 2)), dma((4, 2)), dma((3, 2)), dma((3, 2)), dma((NXY,)), dma((NXY,)),
     ]
     vmem = pl.BlockSpec(memory_space=pltpu.VMEM)
@@ -638,10 +648,10 @@
         kernel,
         out_shape=(
             jax.ShapeDtypeStruct((49, ATOMS, 128), BF),
-            jax.ShapeDtypeStruct((SHARD, 128), F32),
+            jax.ShapeDtypeStruct((2 * HALF, 128), F32),
         ),
         in_specs=[vmem] * 4 + [pl.BlockSpec(memory_space=pl.ANY)] * 6,
-        out_specs=(vmem, vmem),
+        out_specs=(pl.BlockSpec(memory_space=pl.ANY),) * 2,
         scratch_shapes=scratch,
         compiler_params=pltpu.CompilerParams(
             collective_id=0, has_side_effects=True, vmem_limit_bytes=67000000
@@ -656,6 +666,15 @@
         jnp.transpose(cotangent, (1, 0, 2)).reshape(784, 128),
         w_zero, w_one, w_two,
     )
+    agg, wgrad = pl.pallas_call(
+        finish,
+        out_shape=(
+            jax.ShapeDtypeStruct((49, ATOMS, 128), BF),
+            jax.ShapeDtypeStruct((SHARD, 128), F32),
+        ),
+        in_specs=[vmem] * 2,
+        out_specs=(vmem, vmem),
+    )(agg, wgrad)
     return jnp.transpose(agg, (1, 0, 2)), wgrad.reshape(SHARD * 128)
 
 

time: 80.6 us -> 77.6 us (0.963)
  local copies, waits for them, and re-layouts: 3.15 us -> 0 us
    unnamed x2 -> x0, local copies, waits for them, and re-layouts: 3.15 us -> none
    pallas_call x0 -> x1, Pallas kernels: none -> 1.71 us  [shards(): pl.pallas_call(finish, out_shape=(jax.ShapeDtypeStruct((49, ATOMS, 128),...]
    pallas_call x1, Pallas kernels: 76.6 us -> 75.2 us  [shards(): pl.pallas_call(kernel, out_shape=(jax.ShapeDtypeStruct((49, ATOMS, 128),...]
where the time goes in v3:
time: 77.6 us; the launch traced here: 77.5 us
  Pallas kernels  76.9 us (99%)
    pallas_call x1, Pallas kernels, shards(): pl.pallas_call(kernel, out_shape=(jax.ShapeDtypeStruct((49, ATOMS, 128),...  75.2 us
    pallas_call x1, Pallas kernels, shards(): pl.pallas_call(finish, out_shape=(jax.ShapeDtypeStruct((49, ATOMS, 128),...  1.71 us

profile of v3, /device:TPU:1, one launch (start us, length us, event | category | flops | bytes accessed | tf_op | source)
XLA Modules:
  0.0 77.5 jit_solution(13750761459470876484)
XLA Ops:
  0.6 75.2 %shard_map.113 = (bf16[49,16,128]{2,1,0:T(8,128)(2,1)}, f32[176,128]{1,0:T(8,128)}) custom-call(s32[1,128]{1,0:T(1,128)} %bitcast.16, s32[1,128]{1,0:T(1,128)} %bitcast.17, s32[1,128]{1,0:T(1,128)} %bitcast.18, s32[1,128]{1,0:T(1,128)} %bitcast.19, bf16[49,29,256]{2,1,0:T(8,128)(2,1)} %bitcast.13, bf16[784,128]{1,0:T(8,128)(2,1)} %bitcast.14, ...), custom_call_target="tpu_custom_call" | custom-call | tf_op jit(solution)/shard_map/pallas_call | solution.py:647
  75.8 1.7 %shard_map.114 = (bf16[49,16,128]{2,1,0:T(8,128)(2,1)}, f32[171,128]{1,0:T(8,128)}) custom-call(bf16[49,16,128]{2,1,0:T(8,128)(2,1)} %get-tuple-element.6.agg_in, f32[176,128]{1,0:T(8,128)} %get-tuple-element.7.wgrad_in), custom_call_target="tpu_custom_call" | custom-call | tf_op jit(solution)/shard_map/pallas_call | solution.py:669

commit v4 on v3

--- a/solution.py
+++ b/solution.py
@@ -34,11 +34,11 @@
 
 DEGREE = kept_degrees()
 KEPT = len(DEGREE)
-WIRE = KEPT + 2
-SPLIT = 21
-CODE = SPLIT - 2
+WIRE = KEPT + 1
+SPLIT = 20
+CODE = SPLIT - 1
 BY_DEGREE = sorted(range(KEPT), key=lambda k: (DEGREE[k], k))
-PLACE = {k: i if i < CODE else i + 2 for i, k in enumerate(BY_DEGREE)}
+PLACE = {k: i if i < CODE else i + 1 for i, k in enumerate(BY_DEGREE)}
 GROUPS = [(0, 7), (7, 6), (13, 6), (19, 5), (24, 5)]
 
 
@@ -164,8 +164,9 @@
         got = lax.dot_general(
             hot.astype(BF), wide.astype(BF), (((1,), (1,)), ((), ())), preferred_element_type=F32
         )
-        for i in range(3):
-            codes[q, i] = got[:, 128 * i : 128 * i + 128].astype(BF)
+        codes[q, 0] = got[:, 0:128].astype(BF)
+        codes[q, 1] = got[:, 128:256].astype(BF)
+        codes[q, 2] = jnp.where(iota((32, 128), 1) < 64, got[:, 0:128], got[:, 256:384]).astype(BF)
 
     for q in range(NZ):
         fall[q, 784:832] = jnp.zeros((48, 128), BF)
@@ -174,11 +175,11 @@
         q = xypeer(i)
         part = pl.ds(0, SPLIT) if piece == 0 else pl.ds(SPLIT, WIRE - SPLIT)
         return remote(
-            sendb.at[step, part, q], recvb.at[part, step, xy], ex_s.at[step], ex_r.at[step], at(q // 4, z, q % 4)
+            sendb.at[step, part, q], recvb.at[part, step, xy], ex_s, ex_r.at[step // 4], at(q // 4, z, q % 4)
         )
 
     def own_copy(step):
-        return pltpu.make_async_copy(sendb.at[step, :, xy], recvb.at[:, step, xy], loc_s.at[step])
+        return pltpu.make_async_copy(sendb.at[step, :, xy], recvb.at[:, step, xy], loc_s.at[step // 4])
 
     def rotate(step, piece, zz):
         rows = pl.ds(pl.multiple_of(zz * 32, 32), 32)
@@ -194,8 +195,7 @@
             for i, k in enumerate(ks):
                 sendb[step, PLACE[k]] = got[32 * i : 32 * i + 32].reshape(NXY, 2, 128)
         if piece == 0:
-            sendb[step, CODE] = codes[zz, 0].reshape(NXY, 2, 128)
-            sendb[step, CODE + 1] = codes[zz, 2].reshape(NXY, 2, 128)
+            sendb[step, CODE] = codes[zz, 2].reshape(NXY, 2, 128)
 
     def send_block(step, piece):
         def go(i, c):
@@ -206,42 +206,30 @@
         if piece:
             own_copy(step).start()
 
-    def whole(step):
-        part = recvb.at[:, step, pl.ds(0, NXY - 1)]
-        return remote(part, part, ex_s.at[step], ex_r.at[step], at(x, z, y))
-
-    def receive_block(step):
-        whole(step).wait_recv()
-        own_copy(step).wait()
+    def receive_half(h):
+        part = recvb.at[:, pl.ds(4 * h, 4), pl.ds(0, NXY - 1)]
+        remote(part, part, ex_s, ex_r.at[h], partner).wait_recv()
+        part = recvb.at[:, pl.ds(4 * h, 4), 0]
+        pltpu.make_async_copy(part, part, loc_s.at[h]).wait()
 
     loads[1].wait()
     pl.semaphore_wait(barrier, 23)
 
     def code_copy(i):
-        return remote(crow.at[z], crow.at[z], code_s.at[i], code_r.at[i], at(x, zpeer(i), y))
-
-    def code_in(i):
-        q = lax.rem(z - i + NZ, NZ)
-        return remote(crow.at[q], crow.at[q], code_s.at[i], code_r.at[i], at(x, zpeer(i), y))
-
-    def send_code(i, c):
+        lane = 0 if i == 1 else 1 if i == NZ - 1 else 2
+        return remote(crow.at[z], crow.at[z], code_s, code_r.at[lane], at(x, zpeer(i), y))
+
+    def code_all(count, lane):
+        part = crow.at[pl.ds(0, count)]
+        return remote(part, part, code_s, code_r.at[lane], partner)
+
+    for i in range(1, NZ):
         code_copy(i).start()
-        return c
-
-    def wait_code(i, c):
-        code_in(i).wait_recv()
-        return c
-
-    def sent_code(i, c):
-        code_copy(i).wait_send()
-        return c
-
-    lax.fori_loop(1, NZ, send_code, 0)
 
     def ring(hop, piece, block, direction):
         dev = at(x, lax.rem(z + direction + NZ, NZ), y)
         part = fall.at[block, pl.ds(400 * piece, 400 - 16 * piece)]
-        return remote(part, part, ring_s.at[hop, piece], ring_r.at[hop, piece], dev)
+        return remote(part, part, ring_s, ring_r.at[hop, piece], dev)
 
     def behind(n):
         return lax.rem(z - sign * n + 2 * NZ, NZ)
@@ -279,7 +267,9 @@
         def rot(k):
             return recvb[k, 4 * h : 4 * h + 4].reshape(128, 128)
 
-        build_rotation(rot(CODE).astype(F32), rot(CODE + 1).astype(F32), table, leftd, [rows])
+        r, c = iota((128, 256), 0), iota((128, 256), 1)
+        parted = dot(rot(CODE), (r == jnp.where(c < 128, 0, 64)).astype(BF))
+        build_rotation(parted[:, 0:128], parted[:, 128:256], table, leftd, [rows])
         for k in range(KEPT):
             w = width(DEGREE[k])
             lo = ATOMS * DEGREE[k] * DEGREE[k]
@@ -296,8 +286,8 @@
             if n < 3:
                 ring(4 + n, piece, ahead(n), -sign).start()
 
-    code_in(1).wait_recv()
-    code_in(NZ - 1).wait_recv()
+    code_all(1, 0).wait_recv()
+    code_all(1, 1).wait_recv()
     prepare([behind(1), ahead(1)])
     for n in range(1, 5):
         for back in (True, False):
@@ -307,16 +297,14 @@
             for piece in range(2):
                 pass_on(n, piece, back)
                 if n == 2 and back and piece == 0:
-                    lax.fori_loop(2, NZ - 1, wait_code, 0)
+                    code_all(5, 2).wait_recv()
                     prepare([behind(2), ahead(2), behind(3), ahead(3), behind(4)])
                 rotate(step, piece, behind(n) if back else ahead(n))
                 send_block(step, piece)
     loads[2].wait()
-    for early in range(4):
-        receive_block(early)
+    receive_half(0)
     half(0)
-    for late in range(4, NZ):
-        receive_block(late)
+    receive_half(1)
     half(1)
 
     def spread(res, base, length, lo, width_):
@@ -365,10 +353,10 @@
         grads(m)
         lax.fori_loop(lo, hi, pack, 0)
         part = pl.ds(lo, hi - lo)
-        swaps.append(remote(pk.at[part], r0.at[part], dp_s.at[m], dp_r.at[m], partner))
+        swaps.append(remote(pk.at[part], r0.at[part], dp_s, dp_r.at[m], partner))
         swaps[m].start()
     for m, (lo, hi) in enumerate(runs):
-        swaps[m].wait()
+        swaps[m].wait_recv()
         lax.fori_loop(lo, hi, merge, 0)
 
     def mixed(k):
@@ -422,15 +410,15 @@
         order = [mod4(q + 2 * sign), mod4(q - sign), mod4(q + sign), q]
         subs.append(order)
         one.append(
-            [remote(s0.at[i, mod4(p + 2 * sign), j], ra.at[i, j], st_s.at[i, 0, n], st_r.at[i, 0, n], move(sign))
+            [remote(s0.at[i, mod4(p + 2 * sign), j], ra.at[i, j], st_s, st_r.at[i, n], move(sign))
              for n, j in enumerate(order)]
         )
         two.append(
-            [remote(s0.at[i, mod4(p - sign), j], rb.at[i, j], st_s.at[i, 1, n], st_r.at[i, 1, n], move(-sign))
+            [remote(s0.at[i, mod4(p - sign), j], rb.at[i, j], st_s, st_r.at[i, 8], move(-sign))
              for n, j in enumerate(order)]
         )
         three.append(
-            [remote(ta.at[i, j], rc.at[i, j], st_s.at[i, 2, n], st_r.at[i, 2, n], move(sign))
+            [remote(ta.at[i, j], rc.at[i, j], st_s, st_r.at[i, 4 + n], move(sign))
              for n, j in enumerate(order)]
         )
     def mod8(v):
@@ -438,11 +426,11 @@
 
     def up(h, j):
         src = sz.at[mod8(z + 4 * sign), pl.ds(8 * j, 8)] if h == 0 else va.at[h - 1, j]
-        return remote(src, ua.at[h, j], ua_s.at[h, j], ua_r.at[h, j], at(x, mod8(z + sign), y))
+        return remote(src, ua.at[h, j], ua_s, ua_r.at[h, j], at(x, mod8(z + sign), y))
 
     def down(h, j):
         src = sz.at[mod8(z - 3 * sign), pl.ds(8 * j, 8)] if h == 0 else vb.at[h - 1, j]
-        return remote(src, ub.at[h, j], ub_s.at[h, j], ub_r.at[h, j], at(x, mod8(z - sign), y))
+        return remote(src, ub.at[h, j], ub_s, ub_r.at[h, j], at(x, mod8(z - sign), y))
 
     def pass_sum(h, j):
         part = pl.ds(8 * j, 8)
@@ -470,14 +458,15 @@
     four, five, six = [], [], []
     for i, p, _, q, move in parts:
         order = subs[i]
-        four.append(remote(s1.at[i, order[0]], ra1.at[i], su_s.at[i, 0], su_r.at[i, 0], move(sign)))
-        five.append(remote(s1.at[i, order[1]], rb1.at[i], su_s.at[i, 1], su_r.at[i, 1], move(-sign)))
-        six.append(remote(ta1.at[i], rc1.at[i], su_s.at[i, 2], su_r.at[i, 2], move(sign)))
+        four.append(remote(s1.at[i, order[0]], ra1.at[i], su_s, su_r.at[i, 0], move(sign)))
+        five.append(remote(s1.at[i, order[1]], rb1.at[i], su_s, su_r.at[i, 1], move(-sign)))
+        six.append(remote(ta1.at[i], rc1.at[i], su_s, su_r.at[i, 2], move(sign)))
 
     def close(n):
         for i, p, *_ in parts:
             j = subs[i][n]
-            two[i][n].wait_recv()
+            if n == 0:
+                remote(rb.at[i], rb.at[i], st_s, st_r.at[i, 8], partner).wait_recv()
             three[i][n].wait_recv()
             s1[i, j] = (s0[i, p, j].astype(F32) + rb[i, j].astype(F32) + rc[i, j].astype(F32)).astype(BF)
             if n == 0:
@@ -519,7 +508,7 @@
 
     def across(i):
         q = xypeer(i)
-        return remote(sz1.at[q], r4.at[i], w_s.at[i], w_r.at[i], at(q // 4, z, q % 4))
+        return remote(sz1.at[q], r4.at[i], w_s, w_r, at(q // 4, z, q % 4))
 
     def across_go(i, c):
         across(i).start()
@@ -536,7 +525,7 @@
 
     def zcopy(a, i):
         q = zpeer(i)
-        return remote(s2.at[a, q], r3.at[a, i], z_s.at[a, i], z_r.at[a, i], at(x, q, y))
+        return remote(s2.at[a, q], r3.at[a, i], z_s, z_r.at[a], at(x, q, y))
 
     for a in range(2):
 
@@ -546,14 +535,16 @@
 
         lax.fori_loop(1, NZ, zgo, 0)
     total = sz1[xy].astype(F32)
+    part = r4.at[pl.ds(1, NXY - 1)]
+    remote(part, part, w_s, w_r, partner).wait()
     for i in range(1, NXY):
-        across(i).wait()
         total = total + r4[i].astype(F32)
     fin[2 * RING : HALF] = total
     for a in range(2):
         total = s2[a, z].astype(F32)
+        part = r3.at[a, pl.ds(1, NZ - 1)]
+        remote(part, part, z_s, z_r.at[a], partner).wait_recv()
         for i in range(1, NZ):
-            zcopy(a, i).wait()
             total = total + r3[a, i].astype(F32)
         fin[RING * a : RING * a + RING] = total
     mine = wgrad.at[pl.ds(pl.multiple_of(HALF * dp, 8), HALF)]
@@ -561,28 +552,16 @@
     last.start()
     store = pltpu.make_async_copy(fin, mine, out_s.at[1])
     store.start()
-    for j in range(2):
-        for h in range(4):
-            up(h, j).wait_send()
-        for h in range(3):
-            down(h, j).wait_send()
-    for n in range(4):
-        for i in range(2):
-            one[i][n].wait_send()
-            two[i][n].wait_send()
-            three[i][n].wait_send()
-    for i in range(2):
-        four[i].wait_send()
-        five[i].wait_send()
-        six[i].wait_send()
-    for piece in range(2):
-        for n in range(4):
-            ring(n, piece, z, sign).wait_send()
-        for n in range(3):
-            ring(4 + n, piece, z, -sign).wait_send()
-    for step in range(NZ):
-        whole(step).wait_send()
-    lax.fori_loop(1, NZ, sent_code, 0)
+    for part, sem in (
+        (ua, ua_s), (ub, ub_s), (s0.at[:, pl.ds(0, 3)], st_s), (s1.at[:, pl.ds(0, 3)], su_s),
+        (s2.at[:, pl.ds(0, NZ - 1)], z_s), (pk, dp_s),
+    ):
+        remote(part, part, sem, f_r, partner).wait_send()
+    gone = fall.at[pl.ds(0, 7), pl.ds(0, 784)]
+    remote(gone, gone, ring_s, ring_r.at[0, 0], partner).wait_send()
+    gone = sendb.at[:, :, pl.ds(0, NXY - 1)]
+    remote(gone, gone, ex_s, ex_r.at[0], partner).wait_send()
+    code_all(7, 0).wait_send()
     store_agg.wait()
     store.wait()
     last.wait()
@@ -632,16 +611,16 @@
         pltpu.VMEM((2, 2, 8, REST, 128), BF),
         pltpu.VMEM((NXY, REST, 128), BF),
         pltpu.VMEM((NXY, REST, 128), BF),
-        dma((NZ,)), dma((NZ,)),
-        dma((7, 2)), dma((7, 2)),
-        dma((NZ,)), dma((NZ,)), dma((NZ,)),
-        dma((3,)), dma((3,)),
-        dma((2, 3, 4)), dma((2, 3, 4)),
-        dma((2, 3)), dma((2, 3)),
-        dma((2, NZ)), dma((2, NZ)),
+        dma, dma((3,)),
+        dma, dma((7, 2)),
+        dma, dma((2,)), dma((2,)),
+        dma, dma((3,)),
+        dma, dma((2, 9)),
+        dma, dma((2, 3)),
+        dma, dma((2,)),
         dma, dma,
         dma((6,)), dma((2,)),
-        dma((4, 2)), dma((4, 2)), dma((3, 2)), dma((3, 2)), dma((NXY,)), dma((NXY,)),
+        dma, dma((4, 2)), dma, dma((3, 2)), dma, dma,
     ]
     vmem = pl.BlockSpec(memory_space=pltpu.VMEM)
     agg, wgrad = pl.pallas_call(

time: 77.6 us -> 75.9 us (0.978)
  Pallas kernels: 76.9 us -> 75.1 us
    pallas_call x1, Pallas kernels: 75.2 us -> 73.4 us  [shards(): pl.pallas_call(kernel, out_shape=(jax.ShapeDtypeStruct((49, ATOMS, 128),...]
where the time goes in v4:
time: 75.9 us; the launch traced here: 75.8 us
  Pallas kernels  75.1 us (99%)
    pallas_call x1, Pallas kernels, shards(): pl.pallas_call(kernel, out_shape=(jax.ShapeDtypeStruct((49, ATOMS, 128),...  73.4 us
    pallas_call x1, Pallas kernels, shards(): pl.pallas_call(finish, out_shape=(jax.ShapeDtypeStruct((49, ATOMS, 128),...  1.71 us

profile of v4, /device:TPU:1, one launch (start us, length us, event | category | flops | bytes accessed | tf_op | source)
XLA Modules:
  0.0 75.8 jit_solution(8180674905060365926)
XLA Ops:
  0.6 73.4 %shard_map.113 = (bf16[49,16,128]{2,1,0:T(8,128)(2,1)}, f32[176,128]{1,0:T(8,128)}) custom-call(s32[1,128]{1,0:T(1,128)} %bitcast.16, s32[1,128]{1,0:T(1,128)} %bitcast.17, s32[1,128]{1,0:T(1,128)} %bitcast.18, s32[1,128]{1,0:T(1,128)} %bitcast.19, bf16[49,29,256]{2,1,0:T(8,128)(2,1)} %bitcast.13, bf16[784,128]{1,0:T(8,128)(2,1)} %bitcast.14, ...), custom_call_target="tpu_custom_call" | custom-call | tf_op jit(solution)/shard_map/pallas_call | solution.py:626
  74.1 1.7 %shard_map.114 = (bf16[49,16,128]{2,1,0:T(8,128)(2,1)}, f32[171,128]{1,0:T(8,128)}) custom-call(bf16[49,16,128]{2,1,0:T(8,128)(2,1)} %get-tuple-element.6.agg_in, f32[176,128]{1,0:T(8,128)} %get-tuple-element.7.wgrad_in), custom_call_target="tpu_custom_call" | custom-call | tf_op jit(solution)/shard_map/pallas_call | solution.py:648

commit v5 on v4

--- a/solution.py
+++ b/solution.py
@@ -118,21 +118,6 @@
     def xypeer(i):
         return lax.rem(xy + i, NXY)
 
-    barrier = pltpu.get_barrier_semaphore()
-
-    def greet_z(i, c):
-        pl.semaphore_signal(barrier, inc=1, device_id=at(x, zpeer(i), y), device_id_type=MESH)
-        return c
-
-    def greet_xy(i, c):
-        q = xypeer(i)
-        pl.semaphore_signal(barrier, inc=1, device_id=at(q // 4, z, q % 4), device_id_type=MESH)
-        return c
-
-    lax.fori_loop(1, NZ, greet_z, 0)
-    lax.fori_loop(1, NXY, greet_xy, 0)
-    pl.semaphore_signal(barrier, inc=1, device_id=partner, device_id_type=MESH)
-
     loads = [
         pltpu.make_async_copy(a, b, in_s.at[i])
         for i, (a, b) in enumerate(
@@ -142,7 +127,24 @@
             ]
         )
     ]
-    for load in loads:
+    loads[1].start()
+
+    barrier = pltpu.get_barrier_semaphore()
+
+    def greet_z(i, c):
+        pl.semaphore_signal(barrier, inc=1, device_id=at(x, zpeer(i), y), device_id_type=MESH)
+        return c
+
+    def greet_xy(i, c):
+        q = xypeer(i)
+        pl.semaphore_signal(barrier, inc=1, device_id=at(q // 4, z, q % 4), device_id_type=MESH)
+        return c
+
+    lax.fori_loop(1, NZ, greet_z, 0)
+    lax.fori_loop(1, NXY, greet_xy, 0)
+    pl.semaphore_signal(barrier, inc=1, device_id=partner, device_id_type=MESH)
+
+    for load in loads[:3:2]:
         load.start()
 
     trow = jnp.broadcast_to(tgt[...], (EDGES, EDGES)).astype(F32)
@@ -198,11 +200,12 @@
             sendb[step, CODE] = codes[zz, 2].reshape(NXY, 2, 128)
 
     def send_block(step, piece):
-        def go(i, c):
-            exchange(step, piece, i).start()
+        def go(h, c):
+            for i in range(1, 6):
+                exchange(step, piece, 5 * h + i).start()
             return c
 
-        lax.fori_loop(1, NXY, go, 0)
+        lax.fori_loop(0, 3, go, 0)
         if piece:
             own_copy(step).start()
 
@@ -249,6 +252,8 @@
     for piece in range(2):
         rotate(0, piece, z)
         send_block(0, piece)
+    for load in loads[3:]:
+        load.start()
     cpad[784:832] = jnp.zeros((48, 128), BF)
 
     def prepare(blocks):
@@ -351,13 +356,13 @@
     swaps = []
     for m, (lo, hi) in enumerate(runs):
         grads(m)
-        lax.fori_loop(lo, hi, pack, 0)
+        lax.fori_loop(lo // 2, hi // 2, lambda h, c: pack(2 * h + 1, pack(2 * h, c)), 0)
         part = pl.ds(lo, hi - lo)
         swaps.append(remote(pk.at[part], r0.at[part], dp_s, dp_r.at[m], partner))
         swaps[m].start()
     for m, (lo, hi) in enumerate(runs):
         swaps[m].wait_recv()
-        lax.fori_loop(lo, hi, merge, 0)
+        lax.fori_loop(lo // 2, hi // 2, lambda h, c: merge(2 * h + 1, merge(2 * h, c)), 0)
 
     def mixed(k):
         return recvb[k].reshape(SLOTS, 128)
@@ -515,6 +520,10 @@
         return c
 
     lax.fori_loop(1, NXY, across_go, 0)
+    def zcopy(a, i):
+        q = zpeer(i)
+        return remote(s2.at[a, q], r3.at[a, i], z_s, z_r.at[a], at(x, q, y))
+
     gather_atoms()
     store_agg = pltpu.make_async_copy(agg, agg_out, out_s.at[0])
     store_agg.start()
@@ -522,18 +531,9 @@
         five[i].wait_recv()
         six[i].wait_recv()
         s2[i] = (s1[i, subs[i][3]].astype(F32) + rb1[i].astype(F32) + rc1[i].astype(F32)).astype(BF)
-
-    def zcopy(a, i):
-        q = zpeer(i)
-        return remote(s2.at[a, q], r3.at[a, i], z_s, z_r.at[a], at(x, q, y))
-
-    for a in range(2):
-
-        def zgo(i, c):
-            zcopy(a, i).start()
-            return c
-
-        lax.fori_loop(1, NZ, zgo, 0)
+        for far in (4, 3, 5, 2, 6, 1, 7):
+            zcopy(i, far).start()
+
     total = sz1[xy].astype(F32)
     part = r4.at[pl.ds(1, NXY - 1)]
     remote(part, part, w_s, w_r, partner).wait()

time: 75.9 us -> 74.6 us (0.983)
  Pallas kernels: 75.1 us -> 73.8 us
    pallas_call x1, Pallas kernels: 73.4 us -> 72.1 us  [shards(): pl.pallas_call(kernel, out_shape=(jax.ShapeDtypeStruct((49, ATOMS, 128),...]
where the time goes in v5:
time: 74.6 us; the launch traced here: 74.5 us
  Pallas kernels  73.8 us (99%)
    pallas_call x1, Pallas kernels, shards(): pl.pallas_call(kernel, out_shape=(jax.ShapeDtypeStruct((49, ATOMS, 128),...  72.1 us
    pallas_call x1, Pallas kernels, shards(): pl.pallas_call(finish, out_shape=(jax.ShapeDtypeStruct((49, ATOMS, 128),...  1.71 us

profile of v5, /device:TPU:1, one launch (start us, length us, event | category | flops | bytes accessed | tf_op | source)
XLA Modules:
  0.0 74.5 jit_solution(13098255607074021798)
XLA Ops:
  0.6 72.1 %shard_map.113 = (bf16[49,16,128]{2,1,0:T(8,128)(2,1)}, f32[176,128]{1,0:T(8,128)}) custom-call(s32[1,128]{1,0:T(1,128)} %bitcast.16, s32[1,128]{1,0:T(1,128)} %bitcast.17, s32[1,128]{1,0:T(1,128)} %bitcast.18, s32[1,128]{1,0:T(1,128)} %bitcast.19, bf16[49,29,256]{2,1,0:T(8,128)(2,1)} %bitcast.13, bf16[784,128]{1,0:T(8,128)(2,1)} %bitcast.14, ...), custom_call_target="tpu_custom_call" | custom-call | tf_op jit(solution)/shard_map/pallas_call | solution.py:626
  72.8 1.7 %shard_map.114 = (bf16[49,16,128]{2,1,0:T(8,128)(2,1)}, f32[171,128]{1,0:T(8,128)}) custom-call(bf16[49,16,128]{2,1,0:T(8,128)(2,1)} %get-tuple-element.6.agg_in, f32[176,128]{1,0:T(8,128)} %get-tuple-element.7.wgrad_in), custom_call_target="tpu_custom_call" | custom-call | tf_op jit(solution)/shard_map/pallas_call | solution.py:648

commit v6 on v5

--- a/solution.py
+++ b/solution.py
@@ -61,7 +61,7 @@
 
 
 def build_table(wig, wk, table):
-    wk[...] = jnp.zeros_like(wk)
+    wk[:, 48:64] = jnp.zeros((KEPT, 16, 256), BF)
     wk[:, 0:49, :] = jnp.swapaxes(wig[...].astype(F32), 0, 1).astype(BF)
     for degree in range(LMAX + 1):
         w = width(degree)
@@ -131,17 +131,15 @@
 
     barrier = pltpu.get_barrier_semaphore()
 
-    def greet_z(i, c):
+    def greet_xy(h, c):
+        for i in range(1, 6):
+            q = xypeer(5 * h + i)
+            pl.semaphore_signal(barrier, inc=1, device_id=at(q // 4, z, q % 4), device_id_type=MESH)
+        return c
+
+    for i in (4, 3, 5, 2, 6, 1, 7):
         pl.semaphore_signal(barrier, inc=1, device_id=at(x, zpeer(i), y), device_id_type=MESH)
-        return c
-
-    def greet_xy(i, c):
-        q = xypeer(i)
-        pl.semaphore_signal(barrier, inc=1, device_id=at(q // 4, z, q % 4), device_id_type=MESH)
-        return c
-
-    lax.fori_loop(1, NZ, greet_z, 0)
-    lax.fori_loop(1, NXY, greet_xy, 0)
+    lax.fori_loop(0, 3, greet_xy, 0)
     pl.semaphore_signal(barrier, inc=1, device_id=partner, device_id_type=MESH)
 
     for load in loads[:3:2]:
@@ -515,11 +513,12 @@
         q = xypeer(i)
         return remote(sz1.at[q], r4.at[i], w_s, w_r, at(q // 4, z, q % 4))
 
-    def across_go(i, c):
-        across(i).start()
+    def across_go(h, c):
+        for i in range(1, 6):
+            across(5 * h + i).start()
         return c
 
-    lax.fori_loop(1, NXY, across_go, 0)
+    lax.fori_loop(0, 3, across_go, 0)
     def zcopy(a, i):
         q = zpeer(i)
         return remote(s2.at[a, q], r3.at[a, i], z_s, z_r.at[a], at(x, q, y))

time: 74.6 us -> 74.6 us (level)
  no operation moved by 1% of the time
where the time goes in v6:
time: 74.6 us; the launch traced here: 74.5 us
  Pallas kernels  73.8 us (99%)
    pallas_call x1, Pallas kernels, shards(): pl.pallas_call(kernel, out_shape=(jax.ShapeDtypeStruct((49, ATOMS, 128),...  72.1 us
    pallas_call x1, Pallas kernels, shards(): pl.pallas_call(finish, out_shape=(jax.ShapeDtypeStruct((49, ATOMS, 128),...  1.71 us

profile of v6, /device:TPU:1, one launch (start us, length us, event | category | flops | bytes accessed | tf_op | source)
XLA Modules:
  0.0 74.5 jit_solution(15851417640103213908)
XLA Ops:
  0.6 72.1 %shard_map.113 = (bf16[49,16,128]{2,1,0:T(8,128)(2,1)}, f32[176,128]{1,0:T(8,128)}) custom-call(s32[1,128]{1,0:T(1,128)} %bitcast.16, s32[1,128]{1,0:T(1,128)} %bitcast.17, s32[1,128]{1,0:T(1,128)} %bitcast.18, s32[1,128]{1,0:T(1,128)} %bitcast.19, bf16[49,29,256]{2,1,0:T(8,128)(2,1)} %bitcast.13, bf16[784,128]{1,0:T(8,128)(2,1)} %bitcast.14, ...), custom_call_target="tpu_custom_call" | custom-call | tf_op jit(solution)/shard_map/pallas_call | solution.py:625
  72.8 1.7 %shard_map.114 = (bf16[49,16,128]{2,1,0:T(8,128)(2,1)}, f32[171,128]{1,0:T(8,128)}) custom-call(bf16[49,16,128]{2,1,0:T(8,128)(2,1)} %get-tuple-element.6.agg_in, f32[176,128]{1,0:T(8,128)} %get-tuple-element.7.wgrad_in), custom_call_target="tpu_custom_call" | custom-call | tf_op jit(solution)/shard_map/pallas_call | solution.py:647
